TPU v7x, 512 devices: a whole 4x8x8 slice. The times are simulated.
512 devices in a mesh: rows: 8 (over z_lo, core), vec: 64 (over x, y, z_hi).
Axes of the slice: x: 4, y: 8, z: 8 (z_hi: 2, z_lo: 4; z = z_hi * 4 + z_lo), core: 2. Of those that a mesh axis runs over, the one named last changes fastest.
Arguments:
- vectors: float32 [512, 32768], P('vec', 'rows'), may hold values from -6 to 6
- tile_table: float32 [16, 128, 128], replicated, may hold values from -0.3125 to 0.3125
- offsets: int32 [256, 3], P('rows'), may hold values from -2 to 2, as said below
- tile_ids: int32 [256, 3], P('rows'), may hold values from 0 to 15
- bounds: float32 [3], replicated, may hold values from -1.9 to 2.3, as said below
Outputs:
- filtered: float32 [512, 32768], P('vec', 'rows')
- gram_matrix: float32 [512, 512], P(('rows', 'vec'))
Inputs may be any that keep to these rules, and one draw needn't show every extreme that they name: offsets[j, 0] is 0 for every row block j; wherever offsets[j, s] = o is not 0 and j + o lies in 0..255, row block j + o has a slot with offset -o and the same tile number, so the Hamiltonian is symmetric. bounds[0] < bounds[1] < bounds[2]; bounds[1] - bounds[0] lies between 0.1 and 0.3, bounds[2] - bounds[1] between 3.0 and 3.6, and bounds[1] + bounds[2] between 0.4 and 1.0.
All inputs are finite; a program needn't handle non-finite values.
Results may differ from a plain program's by a relative error of at most 0.00013.
Values sent between devices are 32-bit elements; how exact they have to be, the bound alone decides.
No kernel may reach another device: no remote copies, remote signals or barrier semaphores. Data moves between devices by JAX's collectives and lax.ppermute only.
A program may use at most 64 MiB of HBM per device.

v0:
```python
import jax
import jax.numpy as jnp
from jax import lax
from jax.sharding import PartitionSpec as P

BLOCK = 128
R = 2
STEPS = 4


def extended_2(array, sides, width):
    for axis, dim in sides:
        size, length = (lax.axis_size(axis), array.shape[dim])
        up = [(i, (i + 1) % size) for i in range(size - 1)]
        down = [(j, i) for i, j in up]
        last = lax.slice_in_dim(array, length - width, length, axis=dim)
        first = lax.slice_in_dim(array, 0, width, axis=dim)
        before = lax.ppermute(last, axis, up)
        after = lax.ppermute(first, axis, down)
        array = jnp.concatenate([before, array, after], axis=dim)
    return array


def band_product(extended, variant_table, metadata, first_block, out_blocks):
    ext_width = extended.shape[0]
    distinct = variant_table.shape[0] // 3
    slot_count = metadata.shape[1] // 2
    block_shift = metadata[first_block : first_block + out_blocks, :slot_count]
    tile_choice = metadata[first_block : first_block + out_blocks, slot_count:]
    tile_kind = jnp.where(block_shift > 0, 0, jnp.where(block_shift < 0, 1, 2)).astype(jnp.int32)
    table_index = tile_choice + distinct * tile_kind
    positions = first_block + jnp.arange(out_blocks, dtype=jnp.int32)
    sources = positions[:, None] + block_shift
    inside = ((sources >= 0) & (sources < ext_width)).astype(jnp.float32)
    clipped = jnp.clip(sources, 0, ext_width - 1)
    group_size = 8

    def one_group(group_items):
        source_index, keep_mask, tile_index = group_items
        incoming_block = extended[source_index] * keep_mask[:, :, None, None]
        selected_entry = variant_table[tile_index]
        return jnp.einsum(
            "gskc,gsdc->gkd",
            incoming_block,
            selected_entry,
            precision=lax.Precision.HIGHEST,
            preferred_element_type=jnp.float32,
        )

    grouped = lax.map(
        one_group,
        (
            clipped.reshape(-1, group_size, slot_count),
            inside.reshape(-1, group_size, slot_count),
            table_index.reshape(-1, group_size, slot_count),
        ),
    )
    return grouped.reshape((out_blocks,) + extended.shape[1:])


def chebyshev(blocks, operate, bounds):
    half_width = (bounds[2] - bounds[1]) / 2
    centre = (bounds[2] + bounds[1]) / 2
    sigma_one = half_width / (bounds[0] - centre)
    sigma_base = 2 / sigma_one
    previous = blocks
    present_vectors = sigma_one / half_width * (operate(blocks) - centre * blocks)
    sigma_now = sigma_one
    for repeat in range(STEPS - 1):
        sigma_next = 1 / (sigma_base - sigma_now)
        advanced = (
            2 * sigma_next / half_width * (operate(present_vectors) - centre * present_vectors)
            - sigma_now * sigma_next * previous
        )
        previous = present_vectors
        present_vectors = advanced
        sigma_now = sigma_next
    return present_vectors


def on_device(vectors, tile_table, offsets, tile_ids, bounds):
    local_vecs = vectors.shape[0]
    local_rows = vectors.shape[1]
    block_count = local_rows // BLOCK
    blocks = vectors.reshape(local_vecs, block_count, BLOCK).transpose(1, 0, 2)
    metadata = jnp.concatenate([offsets, tile_ids], axis=1)
    flipped = tile_table.transpose(0, 2, 1)
    variant_table = jnp.concatenate([tile_table, flipped, (tile_table + flipped) / 2], axis=0)
    padded_meta = jnp.pad(metadata, ((R, R), (0, 0)))

    def apply_locally(field):
        padded = extended_2(field, (("rows", 0),), R)
        return band_product(padded, variant_table, padded_meta, R, block_count)

    filtered_blocks = chebyshev(blocks, apply_locally, bounds)
    filtered = filtered_blocks.transpose(1, 0, 2).reshape(local_vecs, local_rows)
    stacked = lax.all_to_all(filtered, "vec", split_axis=1, concat_axis=0, tiled=True)
    total_vecs = stacked.shape[0]
    all_rows = local_rows * lax.axis_size("rows")
    owner_count = lax.axis_size(("rows", "vec"))
    owned_rows = total_vecs // owner_count
    contract = (((1,), (1,)), ((), ()))
    partial_value = (
        lax.dot_general(
            stacked,
            stacked,
            contract,
            precision=lax.Precision.HIGHEST,
            preferred_element_type=jnp.float32,
        )
        / all_rows
    )
    summed_gram = lax.psum(partial_value, ("rows", "vec"))
    gram_matrix = lax.dynamic_slice_in_dim(
        summed_gram, lax.axis_index(("rows", "vec")) * owned_rows, owned_rows, 0
    )
    return (filtered, gram_matrix)


def solution(mesh):
    placed = (P("vec", "rows"), P(), P("rows", None), P("rows", None), P())
    return jax.shard_map(
        on_device,
        mesh=mesh,
        in_specs=placed,
        out_specs=(P("vec", "rows"), P(("rows", "vec"), None)),
        check_vma=False,
    )
```

profile of v0, /device:TPU:1, one launch (start us, length us, event | category | flops | bytes accessed | tf_op | source)
XLA Modules:
  0.0 477.1 jit_solution(14210082805207283505)
XLA Ops:
  8.0 5.4 %collective-permute-start = (f32[2,8,128]{2,1,0:T(8,128)S(1)}, f32[2,8,128]{2,1,0:T(8,128)S(1)}, u32[]{:S(2)}, u32[]{:S(2)}) collective-permute-start(f32[2,8,128]{2,1,0:T(8,128)S(1)} %get-tuple-element.308), channel_id=1, source_target_pairs={{0,64},{64,128},{128,192},{192,256},{256,320},{320,384},{384,448},... | collective-permute-start | bytes 24584 | tf_op jit(solution)/shard_map/ppermute | solution.py:18
  13.4 4.7 collective-permute-start.1
  27.9 26.8 %while.40 = (s32[]{:T(128)}, f32[4,8,8,128]{3,2,1,0:T(8,128)}, s32[4,8,3]{1,0,2:T(4,128)S(1)}, f32[36,8,128]{2,1,0:T(8,128)S(1)}, f32[4,8,3]{1,2,0:T(4,128)S(1)}...) while((s32[]{:T(128)}, f32[4,8,8,128]{3,2,1,0:T(8,128)}, s32[4,8,3]{1,0,2:T(4,128)S(1)}, ...), condition=%wide.region_1.2_spmd, body=%wide.region_0.1_spmd.sunk | while | flops 37775504 | bytes 5057085 | solution.py:50
  30.8 3.8 fusion.44
  37.5 3.8 fusion.44
  44.2 3.8 fusion.44
  50.9 3.8 fusion.44
  64.7 26.8 %while.41 = (s32[]{:T(128)}, f32[4,8,8,128]{3,2,1,0:T(8,128)}, s32[4,8,3]{1,0,2:T(4,128)S(1)}, f32[36,8,128]{2,1,0:T(8,128)S(1)}, f32[4,8,3]{1,2,0:T(4,128)S(1)}...) while((s32[]{:T(128)}, f32[4,8,8,128]{3,2,1,0:T(8,128)}, s32[4,8,3]{1,0,2:T(4,128)S(1)}, ...), condition=%wide.region_3.4_spmd, body=%wide.region_2.3_spmd.sunk | while | flops 37775504 | bytes 5057085 | solution.py:50
  67.6 3.8 fusion.47
  74.3 3.8 fusion.47
  81.0 3.8 fusion.47
  87.7 3.8 fusion.47
  101.7 26.8 %while.42 = (s32[]{:T(128)}, f32[4,8,8,128]{3,2,1,0:T(8,128)}, s32[4,8,3]{1,0,2:T(4,128)S(1)}, f32[36,8,128]{2,1,0:T(8,128)S(1)}, f32[4,8,3]{1,2,0:T(4,128)S(1)}...) while((s32[]{:T(128)}, f32[4,8,8,128]{3,2,1,0:T(8,128)}, s32[4,8,3]{1,0,2:T(4,128)S(1)}, ...), condition=%wide.region_5.6_spmd, body=%wide.region_4.5_spmd.sunk | while | flops 37775504 | bytes 5057085 | solution.py:50
  104.6 3.8 fusion.50
  111.3 3.8 fusion.50
  118.0 3.8 fusion.50
  124.7 3.8 fusion.50
  139.2 26.8 %while.43 = (s32[]{:T(128)}, f32[4,8,8,128]{3,2,1,0:T(8,128)}, s32[4,8,3]{1,0,2:T(4,128)S(1)}, f32[36,8,128]{2,1,0:T(8,128)S(1)}, f32[4,8,3]{1,2,0:T(4,128)S(1)}...) while((s32[]{:T(128)}, f32[4,8,8,128]{3,2,1,0:T(8,128)}, s32[4,8,3]{1,0,2:T(4,128)S(1)}, ...), condition=%wide.region_7.8_spmd, body=%wide.region_6.7_spmd.sunk | while | flops 37775504 | bytes 5057085 | solution.py:50
  142.1 3.8 fusion.53
  148.8 3.8 fusion.53
  155.5 3.8 fusion.53
  162.2 3.8 fusion.53
  167.5 30.0 %all_to_all.19 = f32[64,1,512]{2,1,0:T(1,128)S(1)} all-to-all(f32[64,1,512]{2,1,0:T(1,128)S(1)} %reshape.378), channel_id=1, replica_groups=mesh['rows'=8,'vec'=64] {'vec'}, dimensions={0} | all-to-all | bytes 262144 | tf_op jit(solution)/shard_map/all_to_all | solution.py:97
  201.1 267.9 %all-reduce.2.cloned.1.call-done = f32[512,512]{1,0:T(8,128)} async-done(((f32[512,512]{1,0:T(8,128)}), f32[512,512]{1,0:T(8,128)}) %all-reduce.2.cloned.1.call-update) | async-done | bytes 1048592 | tf_op jit(solution)/shard_map/psum | solution.py:113
  (252 shorter events, 89.8 us)
Async XLA Ops:
  7.2 12.5 %copy-start = (f32[16,128,128]{2,1,0:T(8,128)S(1)}, f32[16,128,128]{2,1,0:T(8,128)}, u32[]{:S(2)}) copy-start(f32[16,128,128]{2,1,0:T(8,128)} %param.14) | copy-start | bytes 3145732
  7.2 461.8 %all-reduce.2.cloned.1.call-start = ((), (), s32[]{:S(2)}) async-start(), calls=%async_computation.1 | async-start | bytes 2097152 | tf_op jit(solution)/shard_map/psum | solution.py:113
  8.0 19.2 %collective-permute-start = (f32[2,8,128]{2,1,0:T(8,128)S(1)}, f32[2,8,128]{2,1,0:T(8,128)S(1)}, u32[]{:S(2)}, u32[]{:S(2)}) collective-permute-start(f32[2,8,128]{2,1,0:T(8,128)S(1)} %get-tuple-element.308), channel_id=1, source_target_pairs={{0,64},{64,128},{128,192},{192,256},{256,320},{320,384},{384,448},... | collective-permute-start | bytes 24584 | tf_op jit(solution)/shard_map/ppermute | solution.py:18
  13.4 13.8 %collective-permute-start.1 = (f32[2,8,128]{2,1,0:T(8,128)S(1)}, f32[2,8,128]{2,1,0:T(8,128)S(1)}, u32[]{:S(2)}, u32[]{:S(2)}) collective-permute-start(f32[2,8,128]{2,1,0:T(8,128)S(1)} %get-tuple-element.309), channel_id=1, source_target_pairs={{64,0},{128,64},{192,128},{256,192},{320,256},{384,320},{448,384},... | collective-permute-start | bytes 24584 | tf_op jit(solution)/shard_map/ppermute | solution.py:19
  19.6 1.0 copy-start.2
  19.7 1.0 copy-start.9
  19.7 1.0 copy-start.11
  19.7 1.6 copy-start.1
  21.3 1.6 copy-start.10
  21.3 5.9 %copy-start.3 = (f32[8,4096]{1,0:T(8,128)S(1)}, f32[8,4096]{1,0:T(8,128)}, u32[]{:S(2)}) copy-start(f32[8,4096]{1,0:T(8,128)} %param.13) | copy-start | bytes 393220
  55.6 0.7 copy-start.7
  56.3 4.5 collective-permute-start.2
  58.2 5.0 %collective-permute-start.3 = (f32[2,8,128]{2,1,0:T(8,128)S(1)}, f32[2,8,128]{2,1,0:T(8,128)S(1)}, u32[]{:S(2)}, u32[]{:S(2)}) collective-permute-start(f32[2,8,128]{2,1,0:T(8,128)S(1)} %get-tuple-element.307), channel_id=1, source_target_pairs={{64,0},{128,64},{192,128},{256,192},{320,256},{384,320},{448,384},... | collective-permute-start | bytes 24584 | tf_op jit(solution)/shard_map/ppermute | solution.py:19
  92.6 0.7 copy-start.4
  93.2 4.4 collective-permute-start.4
  95.2 5.0 %collective-permute-start.5 = (f32[2,8,128]{2,1,0:T(8,128)S(1)}, f32[2,8,128]{2,1,0:T(8,128)S(1)}, u32[]{:S(2)}, u32[]{:S(2)}) collective-permute-start(f32[2,8,128]{2,1,0:T(8,128)S(1)} %get-tuple-element.305), channel_id=1, source_target_pairs={{64,0},{128,64},{192,128},{256,192},{320,256},{384,320},{448,384},... | collective-permute-start | bytes 24584 | tf_op jit(solution)/shard_map/ppermute | solution.py:19
  129.6 0.6 copy-start.6
  130.3 4.4 collective-permute-start.6
  132.2 5.4 %collective-permute-start.7 = (f32[2,8,128]{2,1,0:T(8,128)S(1)}, f32[2,8,128]{2,1,0:T(8,128)S(1)}, u32[]{:S(2)}, u32[]{:S(2)}) collective-permute-start(f32[2,8,128]{2,1,0:T(8,128)S(1)} %get-tuple-element.303), channel_id=1, source_target_pairs={{64,0},{128,64},{192,128},{256,192},{320,256},{384,320},{448,384},... | collective-permute-start | bytes 24584 | tf_op jit(solution)/shard_map/ppermute | solution.py:19
  139.2 26.8 %copy-start.5 = (f32[32,8,128]{2,1,0:T(8,128)S(1)}, f32[32,8,128]{2,1,0:T(8,128)}, u32[]{:S(2)}) copy-start(f32[32,8,128]{2,1,0:T(8,128)} %copy-done.4) | copy-start | bytes 393220
  167.0 34.0 %copy-start.8 = (f32[32,8,128]{2,1,0:T(8,128)}, f32[32,8,128]{2,1,0:T(8,128)S(1)}, u32[]{:S(2)}) copy-start(f32[32,8,128]{2,1,0:T(8,128)S(1)} %fusion.14) | copy-start | bytes 393220
Sparse Core Ops, SparseCore 0:
  201.2 267.7 all-reduce.1
where the time goes:
time: 478 us; the launch traced here: 477 us
  waiting for transfers between devices  276 us (58%)
  matrix products  62.9 us (13%)
  local copies, waits for them, and re-layouts  57.2 us (12%)
  blocking collectives  30 us (6%)
  starting transfers between devices  23 us (5%)
  between operations  18.1 us (4%)
  other arithmetic  9.89 us (2%)
    psum x1, waiting for transfers between devices, on_device(): summed_gram = lax.psum(partial_value, ('rows', 'vec'))  268 us
    dot_general x16, matrix products, one_group(): jnp.einsum('gskc,gsdc->gkd', incoming_block, selected_entry, precision=la...  60.9 us
    all_to_all x1, blocking collectives, on_device(): lax.all_to_all(filtered, 'vec', split_axis=1, concat_axis=0, tiled=True)  30 us
    gather x16, local copies, waits for them, and re-layouts, one_group(): selected_entry = variant_table[tile_index]  29.5 us
    ppermute x4, starting transfers between devices, extended_2(): after = lax.ppermute(first, axis, down)  11.8 us
    ppermute x4, starting transfers between devices, extended_2(): before = lax.ppermute(last, axis, up)  11.1 us
  transfers between devices with their start and end apart: 9, of which 4 were waited for; matrix products, arithmetic and copies ran while one was open for 1% of the time, Pallas kernels for 0%

commit v1 on v0

v1 whole, which is shorter than its diff:
```python
import jax
import jax.numpy as jnp
from jax import lax
from jax.experimental import pallas as pl
from jax.experimental.pallas import tpu as pltpu
from jax.sharding import Mesh, PartitionSpec as P

BLOCK = 128
STEPS = 4
REACH = 2
HALO = STEPS * REACH
NT = 16
MIB = 1 << 20
ROWS = ("zl", "core")
VEC = ("x", "y", "zh")


def split(value):
    high = value.astype(jnp.bfloat16).astype(jnp.float32)
    return high, value - high


def table_kernel(tiles_ref, table_ref):
    for tile in range(NT):
        straight = tiles_ref[tile]
        flipped = straight.T
        for kind, matrix in enumerate((flipped, straight, (straight + flipped) / 2)):
            high, low = split(matrix)
            entry = tile + NT * kind
            table_ref[entry, :, :BLOCK] = high.astype(jnp.bfloat16)
            table_ref[entry, :, BLOCK:] = low.astype(jnp.bfloat16)


def filter_kernel(
    vectors_ref, before_ref, after_ref, own_ref, table_ref, bounds_ref,
    filtered_ref, outgoing_ref,
    field_a, field_b, field_c, parts_a, parts_b, plan_vector, plan, sem,
):
    vecs = vectors_ref.shape[0]
    count = vectors_ref.shape[1] // BLOCK
    extent = count + 2 * HALO
    edge = HALO * BLOCK

    lane = lax.broadcasted_iota(jnp.int32, (8, 128), 1)
    row = lax.broadcasted_iota(jnp.int32, (8, 128), 0)
    left = pltpu.roll(before_ref[:, edge:], 128 - (count - HALO), 1)
    own = pltpu.roll(own_ref[...], HALO, 1)
    right = pltpu.roll(after_ref[:, edge:], HALO + count, 1)
    meta = jnp.where(lane < HALO, left, jnp.where(lane < HALO + count, own, right))
    meta = meta.astype(jnp.int32)
    shift = pltpu.roll(meta, 3, 0)
    kind = jnp.where(shift > 0, 0, jnp.where(shift < 0, NT, 2 * NT))
    plan_vector[...] = jnp.where(row < 3, meta + lane, meta + kind)
    copy = pltpu.make_async_copy(plan_vector, plan, sem)
    copy.start()

    def store_parts(target, block, value):
        high, low = split(value)
        target[block] = jnp.concatenate([high, low], axis=0).astype(jnp.bfloat16)

    for block in range(extent):
        if block < HALO:
            value = before_ref[:, block * BLOCK : (block + 1) * BLOCK]
        elif block < HALO + count:
            at = (block - HALO) * BLOCK
            value = vectors_ref[:, at : at + BLOCK]
        else:
            at = (block - HALO - count) * BLOCK
            value = after_ref[:, at : at + BLOCK]
        field_a[block] = value
        store_parts(parts_a, block, value)

    lowest, low_end, high_end = bounds_ref[0], bounds_ref[1], bounds_ref[2]

    def spread(value):
        return jnp.full((vecs, BLOCK), value, jnp.float32)

    half_width = spread((high_end - low_end) * 0.5)
    centre = spread((high_end + low_end) * 0.5)
    sigma_one = half_width / (spread(lowest) - centre)
    sigma_base = 2 / sigma_one
    copy.wait()

    def product(parts, block):
        left_parts, right_parts = [], []
        for slot in range(3):
            left_parts.append(parts[plan[slot, block]])
            right_parts.append(table_ref[plan[3 + slot, block]])
        both = lax.dot_general(
            jnp.concatenate(left_parts, axis=1),
            jnp.concatenate(right_parts, axis=0),
            (((1,), (0,)), ((), ())),
            preferred_element_type=jnp.float32,
        )
        return both[:vecs, :BLOCK] + both[vecs:, :BLOCK] + both[:vecs, BLOCK:]

    fields = [field_a, field_b, field_c, field_a]
    parts = [parts_a, parts_b, parts_a, parts_b]
    sigma = sigma_one
    for step in range(1, STEPS + 1):
        source, source_parts = fields[step - 1], parts[step - 1]
        if step == 1:
            scale, drag = sigma_one / half_width, None
        else:
            following = 1 / (sigma_base - sigma)
            scale, drag = 2 * following / half_width, sigma * following
            sigma = following
        first = REACH * step

        def one_block(block):
            value = scale * (product(source_parts, block) - centre * source[block])
            if drag is not None:
                value = value - drag * fields[step - 2][block]
            if step < STEPS:
                fields[step][block] = value
                store_parts(parts[step], block, value)
            else:
                at = block - HALO
                filtered_ref[:, pl.ds(pl.multiple_of(at * BLOCK, BLOCK), BLOCK)] = value
                owner, part = at // 2, at % 2
                for copy_at in range(4):
                    outgoing_ref[
                        copy_at * (count // 2) + owner,
                        :,
                        pl.ds(pl.multiple_of(part * BLOCK, BLOCK), BLOCK),
                    ] = value

        group = 4

        @pl.loop(0, (extent - 2 * first) // group)
        def _(index):
            for inner in range(group):
                one_block(first + index * group + inner)


def gram_kernel(group_ref, stacked_ref, partial_ref, own_high, own_low):
    total = stacked_ref.shape[0]
    group = group_ref[0]
    high, low = split(stacked_ref[...])
    high, low = high.astype(jnp.bfloat16), low.astype(jnp.bfloat16)
    for part in range(8):
        rows = stacked_ref[pl.ds(pl.multiple_of(part * 64 + group * 16, 16), 16), :]
        own, rest = split(rows)
        own_high[part * 16 : (part + 1) * 16, :] = own.astype(jnp.bfloat16)
        own_low[part * 16 : (part + 1) * 16, :] = rest.astype(jnp.bfloat16)
    contract = (((1,), (1,)), ((), ()))

    def multiply(one, other):
        return lax.dot_general(one, other, contract, preferred_element_type=jnp.float32)

    a_high, a_low = own_high[...], own_low[...]
    partial = multiply(a_high, high) + multiply(a_high, low) + multiply(a_low, high)
    count = partial.shape[0]
    pieces = total // BLOCK
    for piece in range(pieces):
        partial_ref[pl.ds(piece, count, stride=pieces), :] = partial[
            :, piece * BLOCK : (piece + 1) * BLOCK
        ]


def on_device(vectors, tile_table, offsets, tile_ids, bounds):
    vecs, local_rows = vectors.shape
    count = local_rows // BLOCK
    extent = count + 2 * HALO
    edge = HALO * BLOCK
    meta = jnp.concatenate([offsets.T, tile_ids.T], axis=0).astype(jnp.float32)
    meta = jnp.pad(meta, ((0, 2), (0, BLOCK - count)))
    size = lax.axis_size(ROWS)
    up = [(i, i + 1) for i in range(size - 1)]
    down = [(j, i) for i, j in up]
    before = lax.ppermute(
        jnp.concatenate([vectors[:, local_rows - edge :], meta], axis=1), ROWS, up
    )
    after = lax.ppermute(jnp.concatenate([vectors[:, :edge], meta], axis=1), ROWS, down)

    vmem = pl.BlockSpec(memory_space=pltpu.VMEM)
    smem = pl.BlockSpec(memory_space=pltpu.SMEM)
    table = pl.pallas_call(
        table_kernel,
        out_shape=jax.ShapeDtypeStruct((3 * NT, BLOCK, 2 * BLOCK), jnp.bfloat16),
        in_specs=[vmem],
        out_specs=vmem,
        compiler_params=pltpu.CompilerParams(vmem_limit_bytes=16 * MIB),
        name="table",
    )(tile_table)

    field = pltpu.VMEM((extent, vecs, BLOCK), jnp.float32)
    parts = pltpu.VMEM((extent, 2 * vecs, BLOCK), jnp.bfloat16)
    filtered, outgoing = pl.pallas_call(
        filter_kernel,
        out_shape=(
            jax.ShapeDtypeStruct((vecs, local_rows), jnp.float32),
            jax.ShapeDtypeStruct((64, vecs, 2 * BLOCK), jnp.float32),
        ),
        in_specs=[vmem, vmem, vmem, vmem, vmem, smem],
        out_specs=(vmem, vmem),
        scratch_shapes=[
            field, field, field, parts, parts,
            pltpu.VMEM((8, BLOCK), jnp.int32),
            pltpu.SMEM((8, BLOCK), jnp.int32),
            pltpu.SemaphoreType.DMA(()),
        ],
        compiler_params=pltpu.CompilerParams(vmem_limit_bytes=16 * MIB),
        name="filter",
    )(vectors, before, after, meta, table, bounds)

    stacked = lax.all_to_all(outgoing, VEC, split_axis=0, concat_axis=0, tiled=True)
    total = 64 * vecs
    stacked = stacked.reshape(total, 2 * BLOCK)
    group = lax.axis_index("x").astype(jnp.int32).reshape(1)
    owned = total // 4
    partial = pl.pallas_call(
        gram_kernel,
        out_shape=jax.ShapeDtypeStruct((owned * (total // BLOCK), BLOCK), jnp.float32),
        in_specs=[smem, vmem],
        out_specs=vmem,
        scratch_shapes=[pltpu.VMEM((owned, 2 * BLOCK), jnp.bfloat16)] * 2,
        compiler_params=pltpu.CompilerParams(vmem_limit_bytes=16 * MIB),
        name="gram",
    )(group, stacked)
    received = lax.all_to_all(
        partial.reshape(owned, 1, total),
        ROWS + ("y", "zh"),
        split_axis=0,
        concat_axis=0,
        tiled=True,
    )
    gram_matrix = jnp.sum(received, axis=0) / (local_rows * size)
    return filtered, gram_matrix


def solution(mesh):
    fine = Mesh(mesh.devices.reshape(4, 2, 4, 8, 2), ROWS + VEC)
    placed = (P(VEC, ROWS), P(), P(ROWS, None), P(ROWS, None), P())
    return jax.shard_map(
        on_device,
        mesh=fine,
        in_specs=placed,
        out_specs=(P(VEC, ROWS), P(ROWS + VEC, None)),
        check_vma=False,
    )
```

time: 478 us -> 87 us (0.18)
  waiting for transfers between devices: 276 us -> 20.4 us
  matrix products: 62.9 us -> 0 us
  local copies, waits for them, and re-layouts: 57.2 us -> 2.05 us
  between operations: 18.1 us -> 0.74 us
  Pallas kernels: 0 us -> 11.7 us
  other arithmetic: 9.89 us -> 1.51 us
  blocking collectives: 30 us -> 23.6 us
    psum x1 -> x0, waiting for transfers between devices: 268 us -> none  [on_device(): summed_gram = lax.psum(partial_value, ('rows', 'vec'))]
    dot_general x17 -> x0, matrix products: 62.9 us -> none  [the longest x16 60.9 us: one_group(): jnp.einsum('gskc,gsdc->gkd', incoming_block, selected_entry, precision=la...]
    gather x32 -> x0, local copies, waits for them, and re-layouts: 38.8 us -> none  [the longest x16 29.5 us: one_group(): selected_entry = variant_table[tile_index]]
    all_to_all x0 -> x1, waiting for transfers between devices: none -> 20.4 us  [on_device(): lax.all_to_all(outgoing, VEC, split_axis=0, concat_axis=0, tiled=True)]
    all_to_all x0 -> x1, starting transfers between devices: none -> 16.6 us  [on_device(): lax.all_to_all(outgoing, VEC, split_axis=0, concat_axis=0, tiled=True)]
    ppermute x8 -> x2, starting transfers between devices: 23 us -> 10 us  [the longest x1 5.38 us: on_device(): lax.ppermute(jnp.concatenate([vectors[:, local_rows - edge:], meta], axis...]
    pallas_call x0 -> x3, Pallas kernels: none -> 11.7 us  [the longest x1 10.8 us: on_device(): pl.pallas_call(filter_kernel, out_shape=(jax.ShapeDtypeStruct((vecs, loca...]
    ppermute x8 -> x2, waiting for transfers between devices: 7.79 us -> 0.01 us  [the longest x1 0.01 us: on_device(): lax.ppermute(jnp.concatenate([vectors[:, local_rows - edge:], meta], axis...]
  transfers between devices with their start and end apart: 9 -> 3, of which waited for: 4 -> 1; matrix products, arithmetic and copies ran while one was open for 1% -> 0% of each run, Pallas kernels for 0% -> 1%
where the time goes in v1:
time: 87 us; the launch traced here: 86.7 us
  starting transfers between devices  26.7 us (31%)
  blocking collectives  23.6 us (27%)
  waiting for transfers between devices  20.4 us (23%)
  Pallas kernels  11.7 us (13%)
  local copies, waits for them, and re-layouts  2.05 us (2%)
  other arithmetic  1.51 us (2%)
    all_to_all x1, blocking collectives, on_device(): lax.all_to_all(partial.reshape(owned, 1, total), ROWS + ('y', 'zh'), spli...  23.6 us
    all_to_all x1, waiting for transfers between devices, on_device(): lax.all_to_all(outgoing, VEC, split_axis=0, concat_axis=0, tiled=True)  20.4 us
    all_to_all x1, starting transfers between devices, on_device(): lax.all_to_all(outgoing, VEC, split_axis=0, concat_axis=0, tiled=True)  16.6 us
    pallas_call x1, Pallas kernels, on_device(): pl.pallas_call(filter_kernel, out_shape=(jax.ShapeDtypeStruct((vecs, loca...  10.8 us
    ppermute x1, starting transfers between devices, on_device(): lax.ppermute(jnp.concatenate([vectors[:, local_rows - edge:], meta], axis...  5.38 us
    ppermute x1, starting transfers between devices, on_device(): lax.ppermute(jnp.concatenate([vectors[:, :edge], meta], axis=1), ROWS, down)  4.66 us
  transfers between devices with their start and end apart: 3, of which 1 were waited for; matrix products, arithmetic and copies ran while one was open for 0% of the time, Pallas kernels for 1%

profile of v1, /device:TPU:1, one launch (start us, length us, event | category | flops | bytes accessed | tf_op | source)
XLA Modules:
  0.0 86.7 jit_solution(8240903091011118640)
XLA Ops:
  0.6 0.0 copy-start.1
  0.6 0.0 copy-start.2
  0.6 0.8 fusion
  1.5 0.7 add_convert_fusion
  2.2 5.4 %collective-permute-start = (f32[8,1152]{1,0:T(8,128)S(1)}, f32[8,1152]{1,0:T(8,128)S(1)}, u32[]{:S(2)}, u32[]{:S(2)}) collective-permute-start(f32[8,1152]{1,0:T(8,128)S(1)} %get-tuple-element.9), channel_id=1, source_target_pairs={{0,64},{64,128},{128,192},{192,256},{256,320},{320,384},{384,448},... | collective-permute-start | bytes 110600 | tf_op jit(solution)/shard_map/ppermute | solution.py:171
  7.6 4.7 %collective-permute-start.1 = (f32[8,1152]{1,0:T(8,128)S(1)}, f32[8,1152]{1,0:T(8,128)S(1)}, u32[]{:S(2)}, u32[]{:S(2)}) collective-permute-start(f32[8,1152]{1,0:T(8,128)S(1)} %get-tuple-element.8), channel_id=1, source_target_pairs={{64,0},{128,64},{192,128},{256,192},{320,256},{384,320},{448,384},... | collective-permute-start | bytes 110600 | tf_op jit(solution)/shard_map/ppermute | solution.py:174
  12.3 0.0 copy-start
  12.3 1.2 %copy-done = f32[16,128,128]{2,1,0:T(8,128)S(1)} copy-done((f32[16,128,128]{2,1,0:T(8,128)S(1)}, f32[16,128,128]{2,1,0:T(8,128)}, u32[]{:S(2)}) %copy-start) | copy-done | bytes 1048600
  13.5 0.6 table.1.table_ref
  14.0 0.0 collective-permute-done.before_ref
  14.1 0.0 collective-permute-done.1.after_ref
  14.1 0.0 copy-done.1
  14.1 0.0 copy-done.2
  14.1 10.8 %filter.1 = (f32[8,4096]{1,0:T(8,128)}, f32[64,8,256]{2,1,0:T(8,128)}) custom-call(f32[8,4096]{1,0:T(8,128)S(1)} %copy-done.1, f32[8,1152]{1,0:T(8,128)S(1)} %collective-permute-done.before_ref, f32[8,1152]{1,0:T(8,128)S(1)} %collective-permute-done.1.after_ref, f32[8,128]{1,0:T(8,128)S(1)} %pad.4.own_ref, bf16[48,128,256]{2,1,0:T(8,128)(2,1)S(1)} %table.1.table_ref, ...), custom_call_target="tpu_custom_call" | custom-call | tf_op jit(solution)/shard_map/filter/pallas_call | solution.py:189
  24.9 16.6 %all-to-all-start = ((f32[64,8,256]{2,1,0:T(8,128)}), f32[64,8,256]{2,1,0:T(8,128)S(1)}, u32[]{:S(2)}, u32[]{:S(2)}) async-start(f32[64,8,256]{2,1,0:T(8,128)} %get-tuple-element.5), calls=%async_computation | async-start | bytes 1048576 | tf_op jit(solution)/shard_map/all_to_all | solution.py:207
  41.5 20.4 %all-to-all-done = f32[64,8,256]{2,1,0:T(8,128)S(1)} async-done(((f32[64,8,256]{2,1,0:T(8,128)}), f32[64,8,256]{2,1,0:T(8,128)S(1)}, u32[]{:S(2)}, u32[]{:S(2)}) %all-to-all-start) | async-done | bytes 524320 | tf_op jit(solution)/shard_map/all_to_all | solution.py:207
  61.9 0.4 gram.1
  62.3 23.6 %all_to_all.10 = f32[128,1,512]{2,1,0:T(1,128)S(1)} all-to-all(f32[128,1,512]{2,1,0:T(1,128)S(1)} %bitcast.7), channel_id=1, replica_groups=mesh['zl'=4,'core'=2,'x'=4,'y'=8,'zh'=2] {'zl','core','y','zh'}, dimensions={0} | all-to-all | bytes 524288 | tf_op jit(solution)/shard_map/all_to_all | solution.py:221
  85.9 0.2 reduce_sum.9
  86.1 0.6 broadcast_multiply_fusion
  (2 shorter events, 0.0 us)
Async XLA Ops:
  0.6 13.4 %copy-start.1 = (f32[8,4096]{1,0:T(8,128)S(1)}, f32[8,4096]{1,0:T(8,128)}, u32[]{:S(2)}) copy-start(f32[8,4096]{1,0:T(8,128)} %vectors_ref.1) | copy-start | bytes 393220
  0.6 13.4 %copy-start.2 = (f32[3]{0:T(128)S(1)}, f32[3]{0:T(128)}, u32[]{:S(2)}) copy-start(f32[3]{0:T(128)} %bounds_ref.1) | copy-start | bytes 40
  2.2 11.8 %collective-permute-start = (f32[8,1152]{1,0:T(8,128)S(1)}, f32[8,1152]{1,0:T(8,128)S(1)}, u32[]{:S(2)}, u32[]{:S(2)}) collective-permute-start(f32[8,1152]{1,0:T(8,128)S(1)} %get-tuple-element.9), channel_id=1, source_target_pairs={{0,64},{64,128},{128,192},{192,256},{256,320},{320,384},{384,448},... | collective-permute-start | bytes 110600 | tf_op jit(solution)/shard_map/ppermute | solution.py:171
  7.6 6.5 %collective-permute-start.1 = (f32[8,1152]{1,0:T(8,128)S(1)}, f32[8,1152]{1,0:T(8,128)S(1)}, u32[]{:S(2)}, u32[]{:S(2)}) collective-permute-start(f32[8,1152]{1,0:T(8,128)S(1)} %get-tuple-element.8), channel_id=1, source_target_pairs={{64,0},{128,64},{192,128},{256,192},{320,256},{384,320},{448,384},... | collective-permute-start | bytes 110600 | tf_op jit(solution)/shard_map/ppermute | solution.py:174
  12.3 1.2 %copy-start = (f32[16,128,128]{2,1,0:T(8,128)S(1)}, f32[16,128,128]{2,1,0:T(8,128)}, u32[]{:S(2)}) copy-start(f32[16,128,128]{2,1,0:T(8,128)} %tiles_ref.1) | copy-start | bytes 3145732
  24.9 37.0 %all-to-all-start = ((f32[64,8,256]{2,1,0:T(8,128)}), f32[64,8,256]{2,1,0:T(8,128)S(1)}, u32[]{:S(2)}, u32[]{:S(2)}) async-start(f32[64,8,256]{2,1,0:T(8,128)} %get-tuple-element.5), calls=%async_computation | async-start | bytes 1048576 | tf_op jit(solution)/shard_map/all_to_all | solution.py:207

commit v2 on v1

--- a/solution.py
+++ b/solution.py
@@ -133,9 +133,9 @@
                 one_block(first + index * group + inner)
 
 
-def gram_kernel(group_ref, stacked_ref, partial_ref, own_high, own_low):
+def gram_kernel(stacked_ref, partial_ref, own_high, own_low):
     total = stacked_ref.shape[0]
-    group = group_ref[0]
+    group = lax.axis_index("x")
     high, low = split(stacked_ref[...])
     high, low = high.astype(jnp.bfloat16), low.astype(jnp.bfloat16)
     for part in range(8):
@@ -207,17 +207,16 @@
     stacked = lax.all_to_all(outgoing, VEC, split_axis=0, concat_axis=0, tiled=True)
     total = 64 * vecs
     stacked = stacked.reshape(total, 2 * BLOCK)
-    group = lax.axis_index("x").astype(jnp.int32).reshape(1)
     owned = total // 4
     partial = pl.pallas_call(
         gram_kernel,
         out_shape=jax.ShapeDtypeStruct((owned * (total // BLOCK), BLOCK), jnp.float32),
-        in_specs=[smem, vmem],
+        in_specs=[vmem],
         out_specs=vmem,
         scratch_shapes=[pltpu.VMEM((owned, 2 * BLOCK), jnp.bfloat16)] * 2,
         compiler_params=pltpu.CompilerParams(vmem_limit_bytes=16 * MIB),
         name="gram",
-    )(group, stacked)
+    )(stacked)
     received = lax.all_to_all(
         partial.reshape(owned, 1, total),
         ROWS + ("y", "zh"),

time: 87 us -> 85.3 us (0.980)
  blocking collectives: 23.6 us -> 58.6 us
  waiting for transfers between devices: 20.4 us -> 0.01 us
  starting transfers between devices: 26.7 us -> 10.7 us
    all_to_all x0 -> x1, blocking collectives: none -> 35.7 us  [on_device(): lax.all_to_all(outgoing, VEC, split_axis=0, concat_axis=0, tiled=True)]
    all_to_all x1 -> x0, waiting for transfers between devices: 20.4 us -> none  [on_device(): lax.all_to_all(outgoing, VEC, split_axis=0, concat_axis=0, tiled=True)]
    all_to_all x1 -> x0, starting transfers between devices: 16.6 us -> none  [on_device(): lax.all_to_all(outgoing, VEC, split_axis=0, concat_axis=0, tiled=True)]
    ppermute x1, starting transfers between devices: 4.66 us -> 8.75 us  [on_device(): lax.ppermute(jnp.concatenate([vectors[:, :edge], meta], axis=1), ROWS, down)]
    ppermute x1, starting transfers between devices: 5.38 us -> 1.92 us  [on_device(): lax.ppermute(jnp.concatenate([vectors[:, local_rows - edge:], meta], axis...]
  transfers between devices with their start and end apart: 3 -> 2, of which waited for: 1 -> 0; matrix products, arithmetic and copies ran while one was open for 0% -> 0% of each run, Pallas kernels for 1% -> 1%
where the time goes in v2:
time: 85.3 us; the launch traced here: 85.1 us
  blocking collectives  58.6 us (69%)
  Pallas kernels  11.5 us (13%)
  starting transfers between devices  10.7 us (13%)
  local copies, waits for them, and re-layouts  2.05 us (2%)
  other arithmetic  1.51 us (2%)
    all_to_all x1, blocking collectives, on_device(): lax.all_to_all(outgoing, VEC, split_axis=0, concat_axis=0, tiled=True)  35.7 us
    all_to_all x1, blocking collectives, on_device(): lax.all_to_all(partial.reshape(owned, 1, total), ROWS + ('y', 'zh'), spli...  22.9 us
    pallas_call x1, Pallas kernels, on_device(): pl.pallas_call(filter_kernel, out_shape=(jax.ShapeDtypeStruct((vecs, loca...  10.6 us
    ppermute x1, starting transfers between devices, on_device(): lax.ppermute(jnp.concatenate([vectors[:, :edge], meta], axis=1), ROWS, down)  8.75 us
    ppermute x1, starting transfers between devices, on_device(): lax.ppermute(jnp.concatenate([vectors[:, local_rows - edge:], meta], axis...  1.92 us
  transfers between devices with their start and end apart: 2, of which 0 were waited for; matrix products, arithmetic and copies ran while one was open for 0% of the time, Pallas kernels for 1%

profile of v2, /device:TPU:1, one launch (start us, length us, event | category | flops | bytes accessed | tf_op | source)
XLA Modules:
  0.0 85.1 jit_solution(16523802640273687259)
XLA Ops:
  0.6 0.0 copy-start.1
  0.6 0.0 copy-start.2
  0.6 0.8 fusion
  1.5 0.7 add_convert_fusion
  2.2 8.7 %collective-permute-start.1 = (f32[8,1152]{1,0:T(8,128)S(1)}, f32[8,1152]{1,0:T(8,128)S(1)}, u32[]{:S(2)}, u32[]{:S(2)}) collective-permute-start(f32[8,1152]{1,0:T(8,128)S(1)} %get-tuple-element.8), channel_id=1, source_target_pairs={{64,0},{128,64},{192,128},{256,192},{320,256},{384,320},{448,384},... | collective-permute-start | bytes 110600 | tf_op jit(solution)/shard_map/ppermute | solution.py:174
  11.0 1.9 %collective-permute-start = (f32[8,1152]{1,0:T(8,128)S(1)}, f32[8,1152]{1,0:T(8,128)S(1)}, u32[]{:S(2)}, u32[]{:S(2)}) collective-permute-start(f32[8,1152]{1,0:T(8,128)S(1)} %get-tuple-element.9), channel_id=1, source_target_pairs={{0,64},{64,128},{128,192},{192,256},{256,320},{320,384},{384,448},... | collective-permute-start | bytes 110600 | tf_op jit(solution)/shard_map/ppermute | solution.py:171
  12.9 0.0 copy-start
  12.9 1.2 %copy-done = f32[16,128,128]{2,1,0:T(8,128)S(1)} copy-done((f32[16,128,128]{2,1,0:T(8,128)S(1)}, f32[16,128,128]{2,1,0:T(8,128)}, u32[]{:S(2)}) %copy-start) | copy-done | bytes 1048600
  14.1 0.6 table.1.table_ref
  14.7 0.0 collective-permute-done.1.after_ref
  14.7 0.0 collective-permute-done.before_ref
  14.7 0.0 copy-done.1
  14.7 0.0 copy-done.2
  14.7 10.6 %filter.1 = (f32[8,4096]{1,0:T(8,128)}, f32[64,8,256]{2,1,0:T(8,128)S(1)}) custom-call(f32[8,4096]{1,0:T(8,128)S(1)} %copy-done.1, f32[8,1152]{1,0:T(8,128)S(1)} %collective-permute-done.before_ref, f32[8,1152]{1,0:T(8,128)S(1)} %collective-permute-done.1.after_ref, f32[8,128]{1,0:T(8,128)S(1)} %pad.4.own_ref, bf16[48,128,256]{2,1,0:T(8,128)(2,1)S(1)} %table.1.table_ref, ...), custom_call_target="tpu_custom_call" | custom-call | tf_op jit(solution)/shard_map/filter/pallas_call | solution.py:189
  25.3 35.7 %all_to_all.10 = f32[64,8,256]{2,1,0:T(8,128)S(1)} all-to-all(f32[64,8,256]{2,1,0:T(8,128)S(1)} %get-tuple-element.5), channel_id=1, replica_groups=mesh['zl'=4,'core'=2,'x'=4,'y'=8,'zh'=2] {'x','y','zh'}, dimensions={0} | all-to-all | bytes 1048576 | tf_op jit(solution)/shard_map/all_to_all | solution.py:207
  61.0 0.4 gram.1
  61.4 22.9 %all_to_all.11 = f32[128,1,512]{2,1,0:T(1,128)S(1)} all-to-all(f32[128,1,512]{2,1,0:T(1,128)S(1)} %bitcast.6), channel_id=1, replica_groups=mesh['zl'=4,'core'=2,'x'=4,'y'=8,'zh'=2] {'zl','core','y','zh'}, dimensions={0} | all-to-all | bytes 524288 | tf_op jit(solution)/shard_map/all_to_all | solution.py:220
  84.3 0.2 reduce_sum.9
  84.5 0.6 broadcast_multiply_fusion
  (2 shorter events, 0.0 us)
Async XLA Ops:
  0.6 14.1 %copy-start.1 = (f32[8,4096]{1,0:T(8,128)S(1)}, f32[8,4096]{1,0:T(8,128)}, u32[]{:S(2)}) copy-start(f32[8,4096]{1,0:T(8,128)} %vectors_ref.1) | copy-start | bytes 393220
  0.6 14.1 %copy-start.2 = (f32[3]{0:T(128)S(1)}, f32[3]{0:T(128)}, u32[]{:S(2)}) copy-start(f32[3]{0:T(128)} %bounds_ref.1) | copy-start | bytes 40
  2.2 12.5 %collective-permute-start.1 = (f32[8,1152]{1,0:T(8,128)S(1)}, f32[8,1152]{1,0:T(8,128)S(1)}, u32[]{:S(2)}, u32[]{:S(2)}) collective-permute-start(f32[8,1152]{1,0:T(8,128)S(1)} %get-tuple-element.8), channel_id=1, source_target_pairs={{64,0},{128,64},{192,128},{256,192},{320,256},{384,320},{448,384},... | collective-permute-start | bytes 110600 | tf_op jit(solution)/shard_map/ppermute | solution.py:174
  11.0 3.7 %collective-permute-start = (f32[8,1152]{1,0:T(8,128)S(1)}, f32[8,1152]{1,0:T(8,128)S(1)}, u32[]{:S(2)}, u32[]{:S(2)}) collective-permute-start(f32[8,1152]{1,0:T(8,128)S(1)} %get-tuple-element.9), channel_id=1, source_target_pairs={{0,64},{64,128},{128,192},{192,256},{256,320},{320,384},{384,448},... | collective-permute-start | bytes 110600 | tf_op jit(solution)/shard_map/ppermute | solution.py:171
  12.9 1.2 %copy-start = (f32[16,128,128]{2,1,0:T(8,128)S(1)}, f32[16,128,128]{2,1,0:T(8,128)}, u32[]{:S(2)}) copy-start(f32[16,128,128]{2,1,0:T(8,128)} %tiles_ref.1) | copy-start | bytes 3145732

commit v3 on v2

--- a/solution.py
+++ b/solution.py
@@ -1,3 +1,5 @@
+import functools
+
 import jax
 import jax.numpy as jnp
 from jax import lax
@@ -20,15 +22,56 @@
     return high, value - high
 
 
-def table_kernel(tiles_ref, table_ref):
+def table_kernel(tiles_ref, table_ref, tiles_here, sems):
+    step = NT // sems.shape[0]
+    copies = [
+        pltpu.make_async_copy(
+            tiles_ref.at[at : at + step], tiles_here.at[at : at + step], sems.at[at // step]
+        )
+        for at in range(0, NT, step)
+    ]
+    for copy in copies:
+        copy.start()
     for tile in range(NT):
-        straight = tiles_ref[tile]
+        if tile % step == 0:
+            copies[tile // step].wait()
+        straight = tiles_here[tile]
         flipped = straight.T
         for kind, matrix in enumerate((flipped, straight, (straight + flipped) / 2)):
             high, low = split(matrix)
             entry = tile + NT * kind
             table_ref[entry, :, :BLOCK] = high.astype(jnp.bfloat16)
             table_ref[entry, :, BLOCK:] = low.astype(jnp.bfloat16)
+
+
+def pack_kernel(
+    vectors_ref, offsets_ref, ids_ref, up_ref, down_ref, own_ref, offsets_here, ids_here, sems
+):
+    edge = up_ref.shape[1] - BLOCK
+    rows = vectors_ref.shape[1]
+    slots, count = offsets_ref.shape
+    copies = [
+        pltpu.make_async_copy(source, target, sems.at[at])
+        for at, (source, target) in enumerate(
+            (
+                (offsets_ref, offsets_here),
+                (ids_ref, ids_here),
+                (vectors_ref.at[:, rows - edge :], up_ref.at[:, :edge]),
+                (vectors_ref.at[:, :edge], down_ref.at[:, :edge]),
+            )
+        )
+    ]
+    for copy in copies:
+        copy.start()
+    own_ref[...] = jnp.zeros_like(own_ref)
+    copies[0].wait()
+    copies[1].wait()
+    own_ref[:slots, :count] = offsets_here[...].astype(jnp.float32)
+    own_ref[slots : 2 * slots, :count] = ids_here[...].astype(jnp.float32)
+    up_ref[:, edge:] = own_ref[...]
+    down_ref[:, edge:] = own_ref[...]
+    copies[2].wait()
+    copies[3].wait()
 
 
 def filter_kernel(
@@ -107,7 +150,7 @@
             sigma = following
         first = REACH * step
 
-        def one_block(block):
+        def one_block(block, owner, part):
             value = scale * (product(source_parts, block) - centre * source[block])
             if drag is not None:
                 value = value - drag * fields[step - 2][block]
@@ -117,23 +160,22 @@
             else:
                 at = block - HALO
                 filtered_ref[:, pl.ds(pl.multiple_of(at * BLOCK, BLOCK), BLOCK)] = value
-                owner, part = at // 2, at % 2
                 for copy_at in range(4):
                     outgoing_ref[
-                        copy_at * (count // 2) + owner,
-                        :,
-                        pl.ds(pl.multiple_of(part * BLOCK, BLOCK), BLOCK),
+                        copy_at * (count // 2) + owner, :, part * BLOCK : (part + 1) * BLOCK
                     ] = value
 
-        group = 4
-
-        @pl.loop(0, (extent - 2 * first) // group)
+        group = (extent - 2 * first) // 2
+
+        @pl.loop(0, 2)
         def _(index):
             for inner in range(group):
-                one_block(first + index * group + inner)
-
-
-def gram_kernel(stacked_ref, partial_ref, own_high, own_low):
+                one_block(
+                    first + index * group + inner, index * (group // 2) + inner // 2, inner % 2
+                )
+
+
+def gram_kernel(scale, stacked_ref, partial_ref, own_high, own_low):
     total = stacked_ref.shape[0]
     group = lax.axis_index("x")
     high, low = split(stacked_ref[...])
@@ -150,6 +192,7 @@
 
     a_high, a_low = own_high[...], own_low[...]
     partial = multiply(a_high, high) + multiply(a_high, low) + multiply(a_low, high)
+    partial = partial * scale
     count = partial.shape[0]
     pieces = total // BLOCK
     for piece in range(pieces):
@@ -163,26 +206,41 @@
     count = local_rows // BLOCK
     extent = count + 2 * HALO
     edge = HALO * BLOCK
-    meta = jnp.concatenate([offsets.T, tile_ids.T], axis=0).astype(jnp.float32)
-    meta = jnp.pad(meta, ((0, 2), (0, BLOCK - count)))
     size = lax.axis_size(ROWS)
     up = [(i, i + 1) for i in range(size - 1)]
     down = [(j, i) for i, j in up]
-    before = lax.ppermute(
-        jnp.concatenate([vectors[:, local_rows - edge :], meta], axis=1), ROWS, up
-    )
-    after = lax.ppermute(jnp.concatenate([vectors[:, :edge], meta], axis=1), ROWS, down)
-
     vmem = pl.BlockSpec(memory_space=pltpu.VMEM)
     smem = pl.BlockSpec(memory_space=pltpu.SMEM)
+    hbm = pl.BlockSpec(memory_space=pltpu.HBM)
+    packed = jax.ShapeDtypeStruct((vecs, edge + BLOCK), jnp.float32)
+    slots = pltpu.VMEM((3, count), jnp.int32)
+    to_upper, to_lower, meta = pl.pallas_call(
+        pack_kernel,
+        out_shape=(packed, packed, jax.ShapeDtypeStruct((8, BLOCK), jnp.float32)),
+        in_specs=[hbm, hbm, hbm],
+        out_specs=(vmem, vmem, vmem),
+        scratch_shapes=[slots, slots, pltpu.SemaphoreType.DMA((4,))],
+        compiler_params=pltpu.CompilerParams(vmem_limit_bytes=4 * MIB),
+        name="pack",
+    )(*(
+        pltpu.with_memory_space_constraint(array, pltpu.HBM)
+        for array in (vectors, offsets.T, tile_ids.T)
+    ))
+    before = lax.ppermute(to_upper, ROWS, up)
+    after = lax.ppermute(to_lower, ROWS, down)
+
     table = pl.pallas_call(
         table_kernel,
         out_shape=jax.ShapeDtypeStruct((3 * NT, BLOCK, 2 * BLOCK), jnp.bfloat16),
-        in_specs=[vmem],
+        in_specs=[hbm],
         out_specs=vmem,
+        scratch_shapes=[
+            pltpu.VMEM(tile_table.shape, jnp.float32),
+            pltpu.SemaphoreType.DMA((4,)),
+        ],
         compiler_params=pltpu.CompilerParams(vmem_limit_bytes=16 * MIB),
         name="table",
-    )(tile_table)
+    )(pltpu.with_memory_space_constraint(tile_table, pltpu.HBM))
 
     field = pltpu.VMEM((extent, vecs, BLOCK), jnp.float32)
     parts = pltpu.VMEM((extent, 2 * vecs, BLOCK), jnp.bfloat16)
@@ -209,7 +267,7 @@
     stacked = stacked.reshape(total, 2 * BLOCK)
     owned = total // 4
     partial = pl.pallas_call(
-        gram_kernel,
+        functools.partial(gram_kernel, 1.0 / (local_rows * size)),
         out_shape=jax.ShapeDtypeStruct((owned * (total // BLOCK), BLOCK), jnp.float32),
         in_specs=[vmem],
         out_specs=vmem,
@@ -224,7 +282,7 @@
         concat_axis=0,
         tiled=True,
     )
-    gram_matrix = jnp.sum(received, axis=0) / (local_rows * size)
+    gram_matrix = jnp.sum(received, axis=0)
     return filtered, gram_matrix
 
 

time: 85.3 us -> 81.9 us (0.960)
  local copies, waits for them, and re-layouts: 2.05 us -> 0.01 us
  blocking collectives: 58.6 us -> 60.4 us
  Pallas kernels: 11.5 us -> 9.74 us
    pallas_call x1, Pallas kernels: 10.6 us -> 6.8 us  [on_device(): pl.pallas_call(filter_kernel, out_shape=(jax.ShapeDtypeStruct((vecs, loca...]
    all_to_all x1, blocking collectives: 35.7 us -> 36.9 us  [on_device(): lax.all_to_all(outgoing, VEC, split_axis=0, concat_axis=0, tiled=True)]
    unnamed x6 -> x4, local copies, waits for them, and re-layouts: 1.23 us -> 0.01 us
    pallas_call x1, Pallas kernels: 0.56 us -> 1.67 us  [on_device(): pl.pallas_call(table_kernel, out_shape=jax.ShapeDtypeStruct((3 * NT, BLOC...]
    pallas_call x1 -> x2, Pallas kernels: 0.39 us -> 1.26 us  [the longest x1 0.88 us: on_device(): pl.pallas_call(pack_kernel, out_shape=(packed, packed, jax.ShapeDtypeStru...]
  transfers between devices with their start and end apart: 2 -> 2, of which waited for: 0 -> 0; matrix products, arithmetic and copies ran while one was open for 0% -> 0% of each run, Pallas kernels for 1% -> 2%
where the time goes in v3:
time: 81.9 us; the launch traced here: 81.7 us
  blocking collectives  60.4 us (74%)
  starting transfers between devices  10 us (12%)
  Pallas kernels  9.74 us (12%)
    all_to_all x1, blocking collectives, on_device(): lax.all_to_all(outgoing, VEC, split_axis=0, concat_axis=0, tiled=True)  36.9 us
    all_to_all x1, blocking collectives, on_device(): lax.all_to_all(partial.reshape(owned, 1, total), ROWS + ('y', 'zh'), spli...  23.5 us
    pallas_call x1, Pallas kernels, on_device(): pl.pallas_call(filter_kernel, out_shape=(jax.ShapeDtypeStruct((vecs, loca...  6.8 us
    ppermute x1, starting transfers between devices, on_device(): before = lax.ppermute(to_upper, ROWS, up)  5.38 us
    ppermute x1, starting transfers between devices, on_device(): after = lax.ppermute(to_lower, ROWS, down)  4.66 us
    pallas_call x1, Pallas kernels, on_device(): pl.pallas_call(table_kernel, out_shape=jax.ShapeDtypeStruct((3 * NT, BLOC...  1.67 us
  transfers between devices with their start and end apart: 2, of which 0 were waited for; matrix products, arithmetic and copies ran while one was open for 0% of the time, Pallas kernels for 2%

profile of v3, /device:TPU:1, one launch (start us, length us, event | category | flops | bytes accessed | tf_op | source)
XLA Modules:
  0.0 81.7 jit_solution(11159213852824872259)
XLA Ops:
  0.6 0.0 copy-start
  0.6 0.0 copy-start.1
  0.7 0.9 %pack.1 = (f32[8,1152]{1,0:T(8,128)S(1)}, f32[8,1152]{1,0:T(8,128)S(1)}, f32[8,128]{1,0:T(8,128)S(1)}) custom-call(f32[8,4096]{1,0:T(8,128)} %vectors_ref.3, s32[3,32]{1,0:T(4,128)} %bitcast.7, s32[3,32]{1,0:T(4,128)} %bitcast.8), custom_call_target="tpu_custom_call" | custom-call | tf_op jit(solution)/shard_map/pack/pallas_call | solution.py:217
  1.5 5.4 %collective-permute-start = (f32[8,1152]{1,0:T(8,128)S(1)}, f32[8,1152]{1,0:T(8,128)S(1)}, u32[]{:S(2)}, u32[]{:S(2)}) collective-permute-start(f32[8,1152]{1,0:T(8,128)S(1)} %get-tuple-element.7), channel_id=1, source_target_pairs={{0,64},{64,128},{128,192},{192,256},{256,320},{320,384},{384,448},... | collective-permute-start | bytes 110600 | tf_op jit(solution)/shard_map/ppermute | solution.py:229
  6.9 4.7 %collective-permute-start.1 = (f32[8,1152]{1,0:T(8,128)S(1)}, f32[8,1152]{1,0:T(8,128)S(1)}, u32[]{:S(2)}, u32[]{:S(2)}) collective-permute-start(f32[8,1152]{1,0:T(8,128)S(1)} %get-tuple-element.8), channel_id=1, source_target_pairs={{64,0},{128,64},{192,128},{256,192},{320,256},{384,320},{448,384},... | collective-permute-start | bytes 110600 | tf_op jit(solution)/shard_map/ppermute | solution.py:230
  11.6 1.7 %table.1.table_ref = bf16[48,128,256]{2,1,0:T(8,128)(2,1)S(1)} custom-call(f32[16,128,128]{2,1,0:T(8,128)} %tiles_ref.1), custom_call_target="tpu_custom_call" | custom-call | tf_op jit(solution)/shard_map/table/pallas_call | solution.py:232
  13.3 0.0 collective-permute-done.before_ref
  13.3 0.0 collective-permute-done.1.after_ref
  13.3 0.0 copy-done
  13.3 0.0 copy-done.1
  13.3 6.8 %filter.1 = (f32[8,4096]{1,0:T(8,128)}, f32[64,8,256]{2,1,0:T(8,128)S(1)}) custom-call(f32[8,4096]{1,0:T(8,128)S(1)} %copy-done, f32[8,1152]{1,0:T(8,128)S(1)} %collective-permute-done.before_ref, f32[8,1152]{1,0:T(8,128)S(1)} %collective-permute-done.1.after_ref, f32[8,128]{1,0:T(8,128)S(1)} %get-tuple-element.9.own_ref, ...), custom_call_target="tpu_custom_call" | custom-call | tf_op jit(solution)/shard_map/filter/pallas_call | solution.py:247
  20.1 36.9 %all_to_all.10 = f32[64,8,256]{2,1,0:T(8,128)S(1)} all-to-all(f32[64,8,256]{2,1,0:T(8,128)S(1)} %get-tuple-element.11), channel_id=1, replica_groups=mesh['zl'=4,'core'=2,'x'=4,'y'=8,'zh'=2] {'x','y','zh'}, dimensions={0} | all-to-all | bytes 1048576 | tf_op jit(solution)/shard_map/all_to_all | solution.py:265
  57.0 0.4 gram.1
  57.4 23.5 %all_to_all.11 = f32[128,1,512]{2,1,0:T(1,128)S(1)} all-to-all(f32[128,1,512]{2,1,0:T(1,128)S(1)} %bitcast.6), channel_id=1, replica_groups=mesh['zl'=4,'core'=2,'x'=4,'y'=8,'zh'=2] {'zl','core','y','zh'}, dimensions={0} | all-to-all | bytes 524288 | tf_op jit(solution)/shard_map/all_to_all | solution.py:278
  80.9 0.8 reduce_sum.11
Async XLA Ops:
  0.6 12.7 %copy-start = (f32[8,4096]{1,0:T(8,128)S(1)}, f32[8,4096]{1,0:T(8,128)}, u32[]{:S(2)}) copy-start(f32[8,4096]{1,0:T(8,128)} %vectors_ref.3) | copy-start | bytes 393220
  0.6 12.7 %copy-start.1 = (f32[3]{0:T(128)S(1)}, f32[3]{0:T(128)}, u32[]{:S(2)}) copy-start(f32[3]{0:T(128)} %bounds_ref.1) | copy-start | bytes 40
  1.5 11.7 %collective-permute-start = (f32[8,1152]{1,0:T(8,128)S(1)}, f32[8,1152]{1,0:T(8,128)S(1)}, u32[]{:S(2)}, u32[]{:S(2)}) collective-permute-start(f32[8,1152]{1,0:T(8,128)S(1)} %get-tuple-element.7), channel_id=1, source_target_pairs={{0,64},{64,128},{128,192},{192,256},{256,320},{320,384},{384,448},... | collective-permute-start | bytes 110600 | tf_op jit(solution)/shard_map/ppermute | solution.py:229
  6.9 6.4 %collective-permute-start.1 = (f32[8,1152]{1,0:T(8,128)S(1)}, f32[8,1152]{1,0:T(8,128)S(1)}, u32[]{:S(2)}, u32[]{:S(2)}) collective-permute-start(f32[8,1152]{1,0:T(8,128)S(1)} %get-tuple-element.8), channel_id=1, source_target_pairs={{64,0},{128,64},{192,128},{256,192},{320,256},{384,320},{448,384},... | collective-permute-start | bytes 110600 | tf_op jit(solution)/shard_map/ppermute | solution.py:230

commit v4 on v3

--- a/solution.py
+++ b/solution.py
@@ -15,6 +15,8 @@
 MIB = 1 << 20
 ROWS = ("zl", "core")
 VEC = ("x", "y", "zh")
+FIRST_TURN = 0b101001
+SECOND_TURN = 0b1101000
 
 
 def split(value):
@@ -170,26 +172,37 @@
         @pl.loop(0, 2)
         def _(index):
             for inner in range(group):
-                one_block(
-                    first + index * group + inner, index * (group // 2) + inner // 2, inner % 2
-                )
-
-
-def gram_kernel(scale, stacked_ref, partial_ref, own_high, own_low):
+                turn = FIRST_TURN % (count // 2)
+                half = group // 2
+                owner = (index ^ (turn // half)) * half + ((inner // 2) ^ (turn % half))
+                one_block(first + index * group + inner, owner, inner % 2)
+
+
+def gram_kernel(scale, stacked_ref, partial_ref, all_high, all_low, own_high, own_low):
     total = stacked_ref.shape[0]
     group = lax.axis_index("x")
-    high, low = split(stacked_ref[...])
-    high, low = high.astype(jnp.bfloat16), low.astype(jnp.bfloat16)
-    for part in range(8):
-        rows = stacked_ref[pl.ds(pl.multiple_of(part * 64 + group * 16, 16), 16), :]
-        own, rest = split(rows)
-        own_high[part * 16 : (part + 1) * 16, :] = own.astype(jnp.bfloat16)
-        own_low[part * 16 : (part + 1) * 16, :] = rest.astype(jnp.bfloat16)
+
+    def arrived(one, other):
+        tiles = [
+            stacked_ref[pl.ds(pl.multiple_of((at ^ FIRST_TURN) * 8, 8), 8), :] for at in (one, other)
+        ]
+        high, low = split(jnp.concatenate(tiles, axis=0))
+        return high.astype(jnp.bfloat16), low.astype(jnp.bfloat16)
+
+    for pair in range(total // 16):
+        rows = slice(pair * 16, (pair + 1) * 16)
+        all_high[rows, :], all_low[rows, :] = arrived(2 * pair, 2 * pair + 1)
+    for slot in range(8):
+        owner = (slot ^ (SECOND_TURN // 16)) * 8 + group * 2
+        swap = (SECOND_TURN % 16) // 8
+        rows = slice(slot * 16, (slot + 1) * 16)
+        own_high[rows, :], own_low[rows, :] = arrived(owner + swap, owner + 1 - swap)
     contract = (((1,), (1,)), ((), ()))
 
     def multiply(one, other):
         return lax.dot_general(one, other, contract, preferred_element_type=jnp.float32)
 
+    high, low = all_high[...], all_low[...]
     a_high, a_low = own_high[...], own_low[...]
     partial = multiply(a_high, high) + multiply(a_high, low) + multiply(a_low, high)
     partial = partial * scale
@@ -262,7 +275,14 @@
         name="filter",
     )(vectors, before, after, meta, table, bounds)
 
-    stacked = lax.all_to_all(outgoing, VEC, split_axis=0, concat_axis=0, tiled=True)
+    stacked = lax.all_to_all(
+        outgoing,
+        VEC,
+        split_axis=0,
+        concat_axis=0,
+        tiled=True,
+        axis_index_groups=[[at ^ FIRST_TURN for at in range(64)]],
+    )
     total = 64 * vecs
     stacked = stacked.reshape(total, 2 * BLOCK)
     owned = total // 4
@@ -271,7 +291,8 @@
         out_shape=jax.ShapeDtypeStruct((owned * (total // BLOCK), BLOCK), jnp.float32),
         in_specs=[vmem],
         out_specs=vmem,
-        scratch_shapes=[pltpu.VMEM((owned, 2 * BLOCK), jnp.bfloat16)] * 2,
+        scratch_shapes=[pltpu.VMEM((total, 2 * BLOCK), jnp.bfloat16)] * 2
+        + [pltpu.VMEM((owned, 2 * BLOCK), jnp.bfloat16)] * 2,
         compiler_params=pltpu.CompilerParams(vmem_limit_bytes=16 * MIB),
         name="gram",
     )(stacked)
@@ -281,6 +302,7 @@
         split_axis=0,
         concat_axis=0,
         tiled=True,
+        axis_index_groups=[[at ^ SECOND_TURN for at in range(owned)]],
     )
     gram_matrix = jnp.sum(received, axis=0)
     return filtered, gram_matrix

time: 81.9 us -> 74.9 us (0.915)
  blocking collectives: 60.4 us -> 53.4 us
    all_to_all x1, blocking collectives: 36.9 us -> 28.6 us  [on_device(): lax.all_to_all(outgoing, VEC, split_axis=0, concat_axis=0, tiled=True, ax...]
    all_to_all x1, blocking collectives: 23.5 us -> 24.8 us  [on_device(): lax.all_to_all(partial.reshape(owned, 1, total), ROWS + ('y', 'zh'), spli...]
where the time goes in v4:
time: 74.9 us; the launch traced here: 74.7 us
  blocking collectives  53.4 us (71%)
  starting transfers between devices  10 us (13%)
  Pallas kernels  9.74 us (13%)
  other arithmetic  0.79 us (1%)
    all_to_all x1, blocking collectives, on_device(): lax.all_to_all(outgoing, VEC, split_axis=0, concat_axis=0, tiled=True, ax...  28.6 us
    all_to_all x1, blocking collectives, on_device(): lax.all_to_all(partial.reshape(owned, 1, total), ROWS + ('y', 'zh'), spli...  24.8 us
    pallas_call x1, Pallas kernels, on_device(): pl.pallas_call(filter_kernel, out_shape=(jax.ShapeDtypeStruct((vecs, loca...  6.81 us
    ppermute x1, starting transfers between devices, on_device(): before = lax.ppermute(to_upper, ROWS, up)  5.38 us
    ppermute x1, starting transfers between devices, on_device(): after = lax.ppermute(to_lower, ROWS, down)  4.66 us
    pallas_call x1, Pallas kernels, on_device(): pl.pallas_call(table_kernel, out_shape=jax.ShapeDtypeStruct((3 * NT, BLOC...  1.67 us
  transfers between devices with their start and end apart: 2, of which 0 were waited for; matrix products, arithmetic and copies ran while one was open for 0% of the time, Pallas kernels for 2%

profile of v4, /device:TPU:1, one launch (start us, length us, event | category | flops | bytes accessed | tf_op | source)
XLA Modules:
  0.0 74.7 jit_solution(1123373096972851600)
XLA Ops:
  0.6 0.0 copy-start
  0.6 0.0 copy-start.1
  0.7 0.9 %pack.1 = (f32[8,1152]{1,0:T(8,128)S(1)}, f32[8,1152]{1,0:T(8,128)S(1)}, f32[8,128]{1,0:T(8,128)S(1)}) custom-call(f32[8,4096]{1,0:T(8,128)} %vectors_ref.3, s32[3,32]{1,0:T(4,128)} %bitcast.7, s32[3,32]{1,0:T(4,128)} %bitcast.8), custom_call_target="tpu_custom_call" | custom-call | tf_op jit(solution)/shard_map/pack/pallas_call | solution.py:230
  1.5 5.4 %collective-permute-start = (f32[8,1152]{1,0:T(8,128)S(1)}, f32[8,1152]{1,0:T(8,128)S(1)}, u32[]{:S(2)}, u32[]{:S(2)}) collective-permute-start(f32[8,1152]{1,0:T(8,128)S(1)} %get-tuple-element.7), channel_id=1, source_target_pairs={{0,64},{64,128},{128,192},{192,256},{256,320},{320,384},{384,448},... | collective-permute-start | bytes 110600 | tf_op jit(solution)/shard_map/ppermute | solution.py:242
  6.9 4.7 %collective-permute-start.1 = (f32[8,1152]{1,0:T(8,128)S(1)}, f32[8,1152]{1,0:T(8,128)S(1)}, u32[]{:S(2)}, u32[]{:S(2)}) collective-permute-start(f32[8,1152]{1,0:T(8,128)S(1)} %get-tuple-element.8), channel_id=1, source_target_pairs={{64,0},{128,64},{192,128},{256,192},{320,256},{384,320},{448,384},... | collective-permute-start | bytes 110600 | tf_op jit(solution)/shard_map/ppermute | solution.py:243
  11.6 1.7 %table.1.table_ref = bf16[48,128,256]{2,1,0:T(8,128)(2,1)S(1)} custom-call(f32[16,128,128]{2,1,0:T(8,128)} %tiles_ref.1), custom_call_target="tpu_custom_call" | custom-call | tf_op jit(solution)/shard_map/table/pallas_call | solution.py:245
  13.3 0.0 collective-permute-done.before_ref
  13.3 0.0 collective-permute-done.1.after_ref
  13.3 0.0 copy-done
  13.3 0.0 copy-done.1
  13.3 6.8 %filter.1 = (f32[8,4096]{1,0:T(8,128)}, f32[64,8,256]{2,1,0:T(8,128)S(1)}) custom-call(f32[8,4096]{1,0:T(8,128)S(1)} %copy-done, f32[8,1152]{1,0:T(8,128)S(1)} %collective-permute-done.before_ref, f32[8,1152]{1,0:T(8,128)S(1)} %collective-permute-done.1.after_ref, f32[8,128]{1,0:T(8,128)S(1)} %get-tuple-element.9.own_ref, ...), custom_call_target="tpu_custom_call" | custom-call | tf_op jit(solution)/shard_map/filter/pallas_call | solution.py:260
  20.1 28.6 %all_to_all.10 = f32[64,8,256]{2,1,0:T(8,128)S(1)} all-to-all(f32[64,8,256]{2,1,0:T(8,128)S(1)} %get-tuple-element.11), channel_id=1, replica_groups={{41,40,43,42,45,44,47,46,33,32,35,34,37,36,39,38,57,56,59,58,61,60,63,6..., dimensions={0} | all-to-all | bytes 1048576 | tf_op jit(solution)/shard_map/all_to_all | solution.py:278
  48.7 0.4 gram.1
  49.1 24.8 %all_to_all.11 = f32[128,1,512]{2,1,0:T(1,128)S(1)} all-to-all(f32[128,1,512]{2,1,0:T(1,128)S(1)} %bitcast.6), channel_id=1, replica_groups={{392,393,394,395,396,397,398,399,384,385,386,387,388,389,390,391,456,45..., dimensions={0} | all-to-all | bytes 524288 | tf_op jit(solution)/shard_map/all_to_all | solution.py:299
  73.9 0.8 %reduce_sum.11 = f32[512]{0:T(512)} reduce(f32[128,1,512]{2,1,0:T(1,128)S(1)} %all_to_all.11, f32[]{:T(128)} %constant.0.clone.1), dimensions={0,1}, to_apply=%region_0.0 | reduce | flops 65024 | bytes 264196 | tf_op jit(solution)/shard_map/reduce_sum | solution.py:307
Async XLA Ops:
  0.6 12.7 %copy-start = (f32[8,4096]{1,0:T(8,128)S(1)}, f32[8,4096]{1,0:T(8,128)}, u32[]{:S(2)}) copy-start(f32[8,4096]{1,0:T(8,128)} %vectors_ref.3) | copy-start | bytes 393220
  0.6 12.7 %copy-start.1 = (f32[3]{0:T(128)S(1)}, f32[3]{0:T(128)}, u32[]{:S(2)}) copy-start(f32[3]{0:T(128)} %bounds_ref.1) | copy-start | bytes 40
  1.5 11.7 %collective-permute-start = (f32[8,1152]{1,0:T(8,128)S(1)}, f32[8,1152]{1,0:T(8,128)S(1)}, u32[]{:S(2)}, u32[]{:S(2)}) collective-permute-start(f32[8,1152]{1,0:T(8,128)S(1)} %get-tuple-element.7), channel_id=1, source_target_pairs={{0,64},{64,128},{128,192},{192,256},{256,320},{320,384},{384,448},... | collective-permute-start | bytes 110600 | tf_op jit(solution)/shard_map/ppermute | solution.py:242
  6.9 6.4 %collective-permute-start.1 = (f32[8,1152]{1,0:T(8,128)S(1)}, f32[8,1152]{1,0:T(8,128)S(1)}, u32[]{:S(2)}, u32[]{:S(2)}) collective-permute-start(f32[8,1152]{1,0:T(8,128)S(1)} %get-tuple-element.8), channel_id=1, source_target_pairs={{64,0},{128,64},{192,128},{256,192},{320,256},{384,320},{448,384},... | collective-permute-start | bytes 110600 | tf_op jit(solution)/shard_map/ppermute | solution.py:243

commit v5 on v4

--- a/solution.py
+++ b/solution.py
@@ -14,7 +14,8 @@
 NT = 16
 MIB = 1 << 20
 ROWS = ("zl", "core")
-VEC = ("x", "y", "zh")
+VEC = ("x", "yq", "yb", "zh")
+OWNERS = ROWS + ("x", "yb", "zh")
 FIRST_TURN = 0b101001
 SECOND_TURN = 0b1101000
 
@@ -162,9 +163,13 @@
             else:
                 at = block - HALO
                 filtered_ref[:, pl.ds(pl.multiple_of(at * BLOCK, BLOCK), BLOCK)] = value
-                for copy_at in range(4):
+                upper, lower = owner
+                for quarter in range(4):
+                    inner = (lower // 4 * 16 + quarter * 4 + lower % 4) ^ (FIRST_TURN % 32)
                     outgoing_ref[
-                        copy_at * (count // 2) + owner, :, part * BLOCK : (part + 1) * BLOCK
+                        (upper ^ (FIRST_TURN // 32)) * 32 + inner,
+                        :,
+                        part * BLOCK : (part + 1) * BLOCK,
                     ] = value
 
         group = (extent - 2 * first) // 2
@@ -172,31 +177,36 @@
         @pl.loop(0, 2)
         def _(index):
             for inner in range(group):
-                turn = FIRST_TURN % (count // 2)
-                half = group // 2
-                owner = (index ^ (turn // half)) * half + ((inner // 2) ^ (turn % half))
-                one_block(first + index * group + inner, owner, inner % 2)
+                one_block(first + index * group + inner, (index, inner // 2), inner % 2)
 
 
 def gram_kernel(scale, stacked_ref, partial_ref, all_high, all_low, own_high, own_low):
     total = stacked_ref.shape[0]
-    group = lax.axis_index("x")
-
-    def arrived(one, other):
-        tiles = [
-            stacked_ref[pl.ds(pl.multiple_of((at ^ FIRST_TURN) * 8, 8), 8), :] for at in (one, other)
-        ]
+    quarter = lax.axis_index("yq")
+
+    def arrived(at):
+        return stacked_ref[pl.ds(pl.multiple_of((at ^ FIRST_TURN) * 8, 8), 8), :]
+
+    def store(high_ref, low_ref, at, tiles):
         high, low = split(jnp.concatenate(tiles, axis=0))
-        return high.astype(jnp.bfloat16), low.astype(jnp.bfloat16)
+        high_ref[at * 16 : (at + 1) * 16, :] = high.astype(jnp.bfloat16)
+        low_ref[at * 16 : (at + 1) * 16, :] = low.astype(jnp.bfloat16)
 
     for pair in range(total // 16):
-        rows = slice(pair * 16, (pair + 1) * 16)
-        all_high[rows, :], all_low[rows, :] = arrived(2 * pair, 2 * pair + 1)
-    for slot in range(8):
-        owner = (slot ^ (SECOND_TURN // 16)) * 8 + group * 2
-        swap = (SECOND_TURN % 16) // 8
-        rows = slice(slot * 16, (slot + 1) * 16)
-        own_high[rows, :], own_low[rows, :] = arrived(owner + swap, owner + 1 - swap)
+        store(all_high, all_low, pair, [arrived(2 * pair), arrived(2 * pair + 1)])
+
+    upper_rows = lax.broadcasted_iota(jnp.int32, (8, stacked_ref.shape[1]), 0) < 4
+    odd = quarter % 2 == 1
+
+    def owned_tile(at):
+        tiles = [arrived((slot ^ (SECOND_TURN // 4)) * 2 + quarter // 2) for slot in (at, at + 1)]
+        turned = [pltpu.roll(tile, 4, 0) for tile in tiles]
+        first = jnp.where(odd, turned[0], tiles[0])
+        second = jnp.where(odd, tiles[1], turned[1])
+        return jnp.where(upper_rows, first, second)
+
+    for quad in range(8):
+        store(own_high, own_low, quad, [owned_tile(4 * quad), owned_tile(4 * quad + 2)])
     contract = (((1,), (1,)), ((), ()))
 
     def multiply(one, other):
@@ -298,7 +308,7 @@
     )(stacked)
     received = lax.all_to_all(
         partial.reshape(owned, 1, total),
-        ROWS + ("y", "zh"),
+        OWNERS,
         split_axis=0,
         concat_axis=0,
         tiled=True,
@@ -309,7 +319,7 @@
 
 
 def solution(mesh):
-    fine = Mesh(mesh.devices.reshape(4, 2, 4, 8, 2), ROWS + VEC)
+    fine = Mesh(mesh.devices.reshape(4, 2, 4, 4, 2, 2), ROWS + VEC)
     placed = (P(VEC, ROWS), P(), P(ROWS, None), P(ROWS, None), P())
     return jax.shard_map(
         on_device,

time: 74.9 us -> 72.9 us (0.973)
  blocking collectives: 53.4 us -> 51.4 us
    all_to_all x1, blocking collectives: 24.8 us -> 22.8 us  [on_device(): lax.all_to_all(partial.reshape(owned, 1, total), OWNERS, split_axis=0, co...]
where the time goes in v5:
time: 72.9 us; the launch traced here: 72.7 us
  blocking collectives  51.4 us (71%)
  starting transfers between devices  10 us (14%)
  Pallas kernels  9.74 us (13%)
  other arithmetic  0.79 us (1%)
  between operations  0.73 us (1%)
    all_to_all x1, blocking collectives, on_device(): lax.all_to_all(outgoing, VEC, split_axis=0, concat_axis=0, tiled=True, ax...  28.6 us
    all_to_all x1, blocking collectives, on_device(): lax.all_to_all(partial.reshape(owned, 1, total), OWNERS, split_axis=0, co...  22.8 us
    pallas_call x1, Pallas kernels, on_device(): pl.pallas_call(filter_kernel, out_shape=(jax.ShapeDtypeStruct((vecs, loca...  6.8 us
    ppermute x1, starting transfers between devices, on_device(): before = lax.ppermute(to_upper, ROWS, up)  5.38 us
    ppermute x1, starting transfers between devices, on_device(): after = lax.ppermute(to_lower, ROWS, down)  4.66 us
    pallas_call x1, Pallas kernels, on_device(): pl.pallas_call(table_kernel, out_shape=jax.ShapeDtypeStruct((3 * NT, BLOC...  1.67 us
  transfers between devices with their start and end apart: 2, of which 0 were waited for; matrix products, arithmetic and copies ran while one was open for 0% of the time, Pallas kernels for 2%

profile of v5, /device:TPU:1, one launch (start us, length us, event | category | flops | bytes accessed | tf_op | source)
XLA Modules:
  0.0 72.7 jit_solution(9689125986988287025)
XLA Ops:
  0.6 0.0 copy-start
  0.6 0.0 copy-start.1
  0.7 0.9 %pack.1 = (f32[8,1152]{1,0:T(8,128)S(1)}, f32[8,1152]{1,0:T(8,128)S(1)}, f32[8,128]{1,0:T(8,128)S(1)}) custom-call(f32[8,4096]{1,0:T(8,128)} %vectors_ref.3, s32[3,32]{1,0:T(4,128)} %bitcast.7, s32[3,32]{1,0:T(4,128)} %bitcast.8), custom_call_target="tpu_custom_call" | custom-call | tf_op jit(solution)/shard_map/pack/pallas_call | solution.py:240
  1.5 5.4 %collective-permute-start = (f32[8,1152]{1,0:T(8,128)S(1)}, f32[8,1152]{1,0:T(8,128)S(1)}, u32[]{:S(2)}, u32[]{:S(2)}) collective-permute-start(f32[8,1152]{1,0:T(8,128)S(1)} %get-tuple-element.7), channel_id=1, source_target_pairs={{0,64},{64,128},{128,192},{192,256},{256,320},{320,384},{384,448},... | collective-permute-start | bytes 110600 | tf_op jit(solution)/shard_map/ppermute | solution.py:252
  6.9 4.7 %collective-permute-start.1 = (f32[8,1152]{1,0:T(8,128)S(1)}, f32[8,1152]{1,0:T(8,128)S(1)}, u32[]{:S(2)}, u32[]{:S(2)}) collective-permute-start(f32[8,1152]{1,0:T(8,128)S(1)} %get-tuple-element.8), channel_id=1, source_target_pairs={{64,0},{128,64},{192,128},{256,192},{320,256},{384,320},{448,384},... | collective-permute-start | bytes 110600 | tf_op jit(solution)/shard_map/ppermute | solution.py:253
  11.6 1.7 %table.1.table_ref = bf16[48,128,256]{2,1,0:T(8,128)(2,1)S(1)} custom-call(f32[16,128,128]{2,1,0:T(8,128)} %tiles_ref.1), custom_call_target="tpu_custom_call" | custom-call | tf_op jit(solution)/shard_map/table/pallas_call | solution.py:255
  13.3 0.0 collective-permute-done.before_ref
  13.3 0.0 collective-permute-done.1.after_ref
  13.3 0.0 copy-done
  13.3 0.0 copy-done.1
  13.3 6.8 %filter.1 = (f32[8,4096]{1,0:T(8,128)}, f32[64,8,256]{2,1,0:T(8,128)S(1)}) custom-call(f32[8,4096]{1,0:T(8,128)S(1)} %copy-done, f32[8,1152]{1,0:T(8,128)S(1)} %collective-permute-done.before_ref, f32[8,1152]{1,0:T(8,128)S(1)} %collective-permute-done.1.after_ref, f32[8,128]{1,0:T(8,128)S(1)} %get-tuple-element.9.own_ref, ...), custom_call_target="tpu_custom_call" | custom-call | tf_op jit(solution)/shard_map/filter/pallas_call | solution.py:270
  20.1 28.6 %all_to_all.10 = f32[64,8,256]{2,1,0:T(8,128)S(1)} all-to-all(f32[64,8,256]{2,1,0:T(8,128)S(1)} %get-tuple-element.11), channel_id=1, replica_groups={{41,40,43,42,45,44,47,46,33,32,35,34,37,36,39,38,57,56,59,58,61,60,63,6..., dimensions={0} | all-to-all | bytes 1048576 | tf_op jit(solution)/shard_map/all_to_all | solution.py:288
  48.7 0.4 gram.1
  49.1 22.8 %all_to_all.11 = f32[128,1,512]{2,1,0:T(1,128)S(1)} all-to-all(f32[128,1,512]{2,1,0:T(1,128)S(1)} %bitcast.6), channel_id=1, replica_groups={{416,417,418,419,432,433,434,435,384,385,386,387,400,401,402,403,480,48..., dimensions={0} | all-to-all | bytes 524288 | tf_op jit(solution)/shard_map/all_to_all | solution.py:309
  71.9 0.8 %reduce_sum.11 = f32[512]{0:T(512)} reduce(f32[128,1,512]{2,1,0:T(1,128)S(1)} %all_to_all.11, f32[]{:T(128)} %constant.0.clone.1), dimensions={0,1}, to_apply=%region_0.0 | reduce | flops 65024 | bytes 264196 | tf_op jit(solution)/shard_map/reduce_sum | solution.py:317
Async XLA Ops:
  0.6 12.7 %copy-start = (f32[8,4096]{1,0:T(8,128)S(1)}, f32[8,4096]{1,0:T(8,128)}, u32[]{:S(2)}) copy-start(f32[8,4096]{1,0:T(8,128)} %vectors_ref.3) | copy-start | bytes 393220
  0.6 12.7 %copy-start.1 = (f32[3]{0:T(128)S(1)}, f32[3]{0:T(128)}, u32[]{:S(2)}) copy-start(f32[3]{0:T(128)} %bounds_ref.1) | copy-start | bytes 40
  1.5 11.7 %collective-permute-start = (f32[8,1152]{1,0:T(8,128)S(1)}, f32[8,1152]{1,0:T(8,128)S(1)}, u32[]{:S(2)}, u32[]{:S(2)}) collective-permute-start(f32[8,1152]{1,0:T(8,128)S(1)} %get-tuple-element.7), channel_id=1, source_target_pairs={{0,64},{64,128},{128,192},{192,256},{256,320},{320,384},{384,448},... | collective-permute-start | bytes 110600 | tf_op jit(solution)/shard_map/ppermute | solution.py:252
  6.9 6.4 %collective-permute-start.1 = (f32[8,1152]{1,0:T(8,128)S(1)}, f32[8,1152]{1,0:T(8,128)S(1)}, u32[]{:S(2)}, u32[]{:S(2)}) collective-permute-start(f32[8,1152]{1,0:T(8,128)S(1)} %get-tuple-element.8), channel_id=1, source_target_pairs={{64,0},{128,64},{192,128},{256,192},{320,256},{384,320},{448,384},... | collective-permute-start | bytes 110600 | tf_op jit(solution)/shard_map/ppermute | solution.py:253

commit v6 on v5

--- a/solution.py
+++ b/solution.py
@@ -16,7 +16,7 @@
 ROWS = ("zl", "core")
 VEC = ("x", "yq", "yb", "zh")
 OWNERS = ROWS + ("x", "yb", "zh")
-FIRST_TURN = 0b101001
+FIRST_TURN = 0b101000
 SECOND_TURN = 0b1101000
 
 
@@ -25,20 +25,9 @@
     return high, value - high
 
 
-def table_kernel(tiles_ref, table_ref, tiles_here, sems):
-    step = NT // sems.shape[0]
-    copies = [
-        pltpu.make_async_copy(
-            tiles_ref.at[at : at + step], tiles_here.at[at : at + step], sems.at[at // step]
-        )
-        for at in range(0, NT, step)
-    ]
-    for copy in copies:
-        copy.start()
+def table_kernel(tiles_ref, table_ref):
     for tile in range(NT):
-        if tile % step == 0:
-            copies[tile // step].wait()
-        straight = tiles_here[tile]
+        straight = tiles_ref[tile]
         flipped = straight.T
         for kind, matrix in enumerate((flipped, straight, (straight + flipped) / 2)):
             high, low = split(matrix)
@@ -48,7 +37,8 @@
 
 
 def pack_kernel(
-    vectors_ref, offsets_ref, ids_ref, up_ref, down_ref, own_ref, offsets_here, ids_here, sems
+    vectors_ref, offsets_ref, ids_ref, tiles_ref,
+    up_ref, down_ref, own_ref, tiles_here, offsets_here, ids_here, sems,
 ):
     edge = up_ref.shape[1] - BLOCK
     rows = vectors_ref.shape[1]
@@ -61,6 +51,7 @@
                 (ids_ref, ids_here),
                 (vectors_ref.at[:, rows - edge :], up_ref.at[:, :edge]),
                 (vectors_ref.at[:, :edge], down_ref.at[:, :edge]),
+                (tiles_ref, tiles_here),
             )
         )
     ]
@@ -73,8 +64,8 @@
     own_ref[slots : 2 * slots, :count] = ids_here[...].astype(jnp.float32)
     up_ref[:, edge:] = own_ref[...]
     down_ref[:, edge:] = own_ref[...]
-    copies[2].wait()
-    copies[3].wait()
+    for copy in copies[2:]:
+        copy.wait()
 
 
 def filter_kernel(
@@ -237,17 +228,22 @@
     hbm = pl.BlockSpec(memory_space=pltpu.HBM)
     packed = jax.ShapeDtypeStruct((vecs, edge + BLOCK), jnp.float32)
     slots = pltpu.VMEM((3, count), jnp.int32)
-    to_upper, to_lower, meta = pl.pallas_call(
+    to_upper, to_lower, meta, tiles = pl.pallas_call(
         pack_kernel,
-        out_shape=(packed, packed, jax.ShapeDtypeStruct((8, BLOCK), jnp.float32)),
-        in_specs=[hbm, hbm, hbm],
-        out_specs=(vmem, vmem, vmem),
-        scratch_shapes=[slots, slots, pltpu.SemaphoreType.DMA((4,))],
+        out_shape=(
+            packed,
+            packed,
+            jax.ShapeDtypeStruct((8, BLOCK), jnp.float32),
+            jax.ShapeDtypeStruct(tile_table.shape, jnp.float32),
+        ),
+        in_specs=[hbm] * 4,
+        out_specs=(vmem,) * 4,
+        scratch_shapes=[slots, slots, pltpu.SemaphoreType.DMA((5,))],
         compiler_params=pltpu.CompilerParams(vmem_limit_bytes=4 * MIB),
         name="pack",
     )(*(
         pltpu.with_memory_space_constraint(array, pltpu.HBM)
-        for array in (vectors, offsets.T, tile_ids.T)
+        for array in (vectors, offsets.T, tile_ids.T, tile_table)
     ))
     before = lax.ppermute(to_upper, ROWS, up)
     after = lax.ppermute(to_lower, ROWS, down)
@@ -255,15 +251,11 @@
     table = pl.pallas_call(
         table_kernel,
         out_shape=jax.ShapeDtypeStruct((3 * NT, BLOCK, 2 * BLOCK), jnp.bfloat16),
-        in_specs=[hbm],
+        in_specs=[vmem],
         out_specs=vmem,
-        scratch_shapes=[
-            pltpu.VMEM(tile_table.shape, jnp.float32),
-            pltpu.SemaphoreType.DMA((4,)),
-        ],
         compiler_params=pltpu.CompilerParams(vmem_limit_bytes=16 * MIB),
         name="table",
-    )(pltpu.with_memory_space_constraint(tile_table, pltpu.HBM))
+    )(tiles)
 
     field = pltpu.VMEM((extent, vecs, BLOCK), jnp.float32)
     parts = pltpu.VMEM((extent, 2 * vecs, BLOCK), jnp.bfloat16)

time: 72.9 us -> 74.3 us (1.019)
  blocking collectives: 51.4 us -> 53.1 us
    all_to_all x1, blocking collectives: 28.6 us -> 34.1 us  [on_device(): lax.all_to_all(outgoing, VEC, split_axis=0, concat_axis=0, tiled=True, ax...]
    all_to_all x1, blocking collectives: 22.8 us -> 19.1 us  [on_device(): lax.all_to_all(partial.reshape(owned, 1, total), OWNERS, split_axis=0, co...]
    pallas_call x1, Pallas kernels: 1.67 us -> 0.56 us  [on_device(): pl.pallas_call(table_kernel, out_shape=jax.ShapeDtypeStruct((3 * NT, BLOC...]
  transfers between devices with their start and end apart: 2 -> 2, of which waited for: 0 -> 1; matrix products, arithmetic and copies ran while one was open for 0% -> 0% of each run, Pallas kernels for 2% -> 1%
where the time goes in v6:
time: 74.3 us; the launch traced here: 74.1 us
  blocking collectives  53.1 us (71%)
  starting transfers between devices  10 us (13%)
  Pallas kernels  9.13 us (12%)
  other arithmetic  0.79 us (1%)
    all_to_all x1, blocking collectives, on_device(): lax.all_to_all(outgoing, VEC, split_axis=0, concat_axis=0, tiled=True, ax...  34.1 us
    all_to_all x1, blocking collectives, on_device(): lax.all_to_all(partial.reshape(owned, 1, total), OWNERS, split_axis=0, co...  19.1 us
    pallas_call x1, Pallas kernels, on_device(): pl.pallas_call(filter_kernel, out_shape=(jax.ShapeDtypeStruct((vecs, loca...  6.8 us
    ppermute x1, starting transfers between devices, on_device(): before = lax.ppermute(to_upper, ROWS, up)  5.38 us
    ppermute x1, starting transfers between devices, on_device(): after = lax.ppermute(to_lower, ROWS, down)  4.66 us
  transfers between devices with their start and end apart: 2, of which 1 were waited for; matrix products, arithmetic and copies ran while one was open for 0% of the time, Pallas kernels for 1%

profile of v6, /device:TPU:1, one launch (start us, length us, event | category | flops | bytes accessed | tf_op | source)
XLA Modules:
  0.0 74.1 jit_solution(8161247773937741927)
XLA Ops:
  0.6 0.0 copy-start
  0.6 0.0 copy-start.1
  0.7 1.4 %pack.1 = (f32[8,1152]{1,0:T(8,128)S(1)}, f32[8,1152]{1,0:T(8,128)S(1)}, f32[8,128]{1,0:T(8,128)S(1)}, f32[16,128,128]{2,1,0:T(8,128)S(1)}) custom-call(f32[8,4096]{1,0:T(8,128)} %vectors_ref.3, s32[3,32]{1,0:T(4,128)} %bitcast.7, s32[3,32]{1,0:T(4,128)} %bitcast.8, f32[16,128,128]{2,1,0:T(8,128)} %tiles_ref.1), custom_call_target="tpu_custom_call" | custom-call | tf_op jit(solution)/shard_map/pack/pallas_call | solution.py:231
  2.0 5.4 %collective-permute-start = (f32[8,1152]{1,0:T(8,128)S(1)}, f32[8,1152]{1,0:T(8,128)S(1)}, u32[]{:S(2)}, u32[]{:S(2)}) collective-permute-start(f32[8,1152]{1,0:T(8,128)S(1)} %get-tuple-element.8), channel_id=1, source_target_pairs={{0,64},{64,128},{128,192},{192,256},{256,320},{320,384},{384,448},... | collective-permute-start | bytes 110600 | tf_op jit(solution)/shard_map/ppermute | solution.py:248
  7.4 4.7 %collective-permute-start.1 = (f32[8,1152]{1,0:T(8,128)S(1)}, f32[8,1152]{1,0:T(8,128)S(1)}, u32[]{:S(2)}, u32[]{:S(2)}) collective-permute-start(f32[8,1152]{1,0:T(8,128)S(1)} %get-tuple-element.9), channel_id=1, source_target_pairs={{64,0},{128,64},{192,128},{256,192},{320,256},{384,320},{448,384},... | collective-permute-start | bytes 110600 | tf_op jit(solution)/shard_map/ppermute | solution.py:249
  12.1 0.6 table.1.table_ref
  12.7 0.0 collective-permute-done.before_ref
  12.7 0.3 collective-permute-done.1.after_ref
  12.9 0.0 copy-done
  12.9 0.0 copy-done.1
  12.9 6.8 %filter.1 = (f32[8,4096]{1,0:T(8,128)}, f32[64,8,256]{2,1,0:T(8,128)S(1)}) custom-call(f32[8,4096]{1,0:T(8,128)S(1)} %copy-done, f32[8,1152]{1,0:T(8,128)S(1)} %collective-permute-done.before_ref, f32[8,1152]{1,0:T(8,128)S(1)} %collective-permute-done.1.after_ref, f32[8,128]{1,0:T(8,128)S(1)} %get-tuple-element.10.own_ref, ...), custom_call_target="tpu_custom_call" | custom-call | tf_op jit(solution)/shard_map/filter/pallas_call | solution.py:262
  19.7 34.1 %all_to_all.10 = f32[64,8,256]{2,1,0:T(8,128)S(1)} all-to-all(f32[64,8,256]{2,1,0:T(8,128)S(1)} %get-tuple-element.13), channel_id=1, replica_groups={{40,41,42,43,44,45,46,47,32,33,34,35,36,37,38,39,56,57,58,59,60,61,62,6..., dimensions={0} | all-to-all | bytes 1048576 | tf_op jit(solution)/shard_map/all_to_all | solution.py:280
  53.8 0.4 gram.1
  54.2 19.1 %all_to_all.11 = f32[128,1,512]{2,1,0:T(1,128)S(1)} all-to-all(f32[128,1,512]{2,1,0:T(1,128)S(1)} %bitcast.6), channel_id=1, replica_groups={{416,417,418,419,432,433,434,435,384,385,386,387,400,401,402,403,480,48..., dimensions={0} | all-to-all | bytes 524288 | tf_op jit(solution)/shard_map/all_to_all | solution.py:301
  73.3 0.8 %reduce_sum.11 = f32[512]{0:T(512)} reduce(f32[128,1,512]{2,1,0:T(1,128)S(1)} %all_to_all.11, f32[]{:T(128)} %constant.0.clone.1), dimensions={0,1}, to_apply=%region_0.0 | reduce | flops 65024 | bytes 264196 | tf_op jit(solution)/shard_map/reduce_sum | solution.py:309
Async XLA Ops:
  0.6 12.3 %copy-start = (f32[8,4096]{1,0:T(8,128)S(1)}, f32[8,4096]{1,0:T(8,128)}, u32[]{:S(2)}) copy-start(f32[8,4096]{1,0:T(8,128)} %vectors_ref.3) | copy-start | bytes 393220
  0.6 12.3 %copy-start.1 = (f32[3]{0:T(128)S(1)}, f32[3]{0:T(128)}, u32[]{:S(2)}) copy-start(f32[3]{0:T(128)} %bounds_ref.1) | copy-start | bytes 40
  2.0 10.6 %collective-permute-start = (f32[8,1152]{1,0:T(8,128)S(1)}, f32[8,1152]{1,0:T(8,128)S(1)}, u32[]{:S(2)}, u32[]{:S(2)}) collective-permute-start(f32[8,1152]{1,0:T(8,128)S(1)} %get-tuple-element.8), channel_id=1, source_target_pairs={{0,64},{64,128},{128,192},{192,256},{256,320},{320,384},{384,448},... | collective-permute-start | bytes 110600 | tf_op jit(solution)/shard_map/ppermute | solution.py:248
  7.4 5.5 %collective-permute-start.1 = (f32[8,1152]{1,0:T(8,128)S(1)}, f32[8,1152]{1,0:T(8,128)S(1)}, u32[]{:S(2)}, u32[]{:S(2)}) collective-permute-start(f32[8,1152]{1,0:T(8,128)S(1)} %get-tuple-element.9), channel_id=1, source_target_pairs={{64,0},{128,64},{192,128},{256,192},{320,256},{384,320},{448,384},... | collective-permute-start | bytes 110600 | tf_op jit(solution)/shard_map/ppermute | solution.py:249

commit v7 on v5

--- a/solution.py
+++ b/solution.py
@@ -48,10 +48,13 @@
 
 
 def pack_kernel(
-    vectors_ref, offsets_ref, ids_ref, up_ref, down_ref, own_ref, offsets_here, ids_here, sems
+    vectors_ref, offsets_ref, ids_ref, mate_ref, cross_ref, own_ref, offsets_here, ids_here, sems
 ):
-    edge = up_ref.shape[1] - BLOCK
-    rows = vectors_ref.shape[1]
+    edge = mate_ref.shape[1] - BLOCK
+    last = vectors_ref.shape[1] - edge
+    core = lax.axis_index("core")
+    to_mate = pl.ds(pl.multiple_of((1 - core) * last, BLOCK), edge)
+    to_cross = pl.ds(pl.multiple_of(core * last, BLOCK), edge)
     slots, count = offsets_ref.shape
     copies = [
         pltpu.make_async_copy(source, target, sems.at[at])
@@ -59,8 +62,8 @@
             (
                 (offsets_ref, offsets_here),
                 (ids_ref, ids_here),
-                (vectors_ref.at[:, rows - edge :], up_ref.at[:, :edge]),
-                (vectors_ref.at[:, :edge], down_ref.at[:, :edge]),
+                (vectors_ref.at[:, to_mate], mate_ref.at[:, :edge]),
+                (vectors_ref.at[:, to_cross], cross_ref.at[:, :edge]),
             )
         )
     ]
@@ -71,14 +74,14 @@
     copies[1].wait()
     own_ref[:slots, :count] = offsets_here[...].astype(jnp.float32)
     own_ref[slots : 2 * slots, :count] = ids_here[...].astype(jnp.float32)
-    up_ref[:, edge:] = own_ref[...]
-    down_ref[:, edge:] = own_ref[...]
+    mate_ref[:, edge:] = own_ref[...]
+    cross_ref[:, edge:] = own_ref[...]
     copies[2].wait()
     copies[3].wait()
 
 
 def filter_kernel(
-    vectors_ref, before_ref, after_ref, own_ref, table_ref, bounds_ref,
+    vectors_ref, mate_ref, cross_ref, own_ref, table_ref, bounds_ref,
     filtered_ref, outgoing_ref,
     field_a, field_b, field_c, parts_a, parts_b, plan_vector, plan, sem,
 ):
@@ -87,11 +90,20 @@
     extent = count + 2 * HALO
     edge = HALO * BLOCK
 
+    upper = lax.axis_index("core") == 1
+
+    def before(at):
+        return jnp.where(upper, mate_ref[:, at], cross_ref[:, at])
+
+    def after(at):
+        return jnp.where(upper, cross_ref[:, at], mate_ref[:, at])
+
+    last = slice(edge, edge + BLOCK)
     lane = lax.broadcasted_iota(jnp.int32, (8, 128), 1)
     row = lax.broadcasted_iota(jnp.int32, (8, 128), 0)
-    left = pltpu.roll(before_ref[:, edge:], 128 - (count - HALO), 1)
+    left = pltpu.roll(before(last), 128 - (count - HALO), 1)
     own = pltpu.roll(own_ref[...], HALO, 1)
-    right = pltpu.roll(after_ref[:, edge:], HALO + count, 1)
+    right = pltpu.roll(after(last), HALO + count, 1)
     meta = jnp.where(lane < HALO, left, jnp.where(lane < HALO + count, own, right))
     meta = meta.astype(jnp.int32)
     shift = pltpu.roll(meta, 3, 0)
@@ -106,13 +118,13 @@
 
     for block in range(extent):
         if block < HALO:
-            value = before_ref[:, block * BLOCK : (block + 1) * BLOCK]
+            value = before(slice(block * BLOCK, (block + 1) * BLOCK))
         elif block < HALO + count:
             at = (block - HALO) * BLOCK
             value = vectors_ref[:, at : at + BLOCK]
         else:
             at = (block - HALO - count) * BLOCK
-            value = after_ref[:, at : at + BLOCK]
+            value = after(slice(at, at + BLOCK))
         field_a[block] = value
         store_parts(parts_a, block, value)
 
@@ -198,12 +210,21 @@
     upper_rows = lax.broadcasted_iota(jnp.int32, (8, stacked_ref.shape[1]), 0) < 4
     odd = quarter % 2 == 1
 
+    row = lax.broadcasted_iota(jnp.int32, (8, stacked_ref.shape[1]), 0)
+
+    def turned_rows(tile):
+        for bit in (1, 2):
+            if SECOND_TURN & bit:
+                back, forth = pltpu.roll(tile, 8 - bit, 0), pltpu.roll(tile, bit, 0)
+                tile = jnp.where(row & bit == 0, back, forth)
+        return tile
+
     def owned_tile(at):
         tiles = [arrived((slot ^ (SECOND_TURN // 4)) * 2 + quarter // 2) for slot in (at, at + 1)]
         turned = [pltpu.roll(tile, 4, 0) for tile in tiles]
         first = jnp.where(odd, turned[0], tiles[0])
         second = jnp.where(odd, tiles[1], turned[1])
-        return jnp.where(upper_rows, first, second)
+        return turned_rows(jnp.where(upper_rows, first, second))
 
     for quad in range(8):
         store(own_high, own_low, quad, [owned_tile(4 * quad), owned_tile(4 * quad + 2)])
@@ -230,14 +251,14 @@
     extent = count + 2 * HALO
     edge = HALO * BLOCK
     size = lax.axis_size(ROWS)
-    up = [(i, i + 1) for i in range(size - 1)]
-    down = [(j, i) for i, j in up]
+    mates = [(i, i ^ 1) for i in range(size)]
+    across = [(i, i + 1 if i % 2 else i - 1) for i in range(1, size - 1)]
     vmem = pl.BlockSpec(memory_space=pltpu.VMEM)
     smem = pl.BlockSpec(memory_space=pltpu.SMEM)
     hbm = pl.BlockSpec(memory_space=pltpu.HBM)
     packed = jax.ShapeDtypeStruct((vecs, edge + BLOCK), jnp.float32)
     slots = pltpu.VMEM((3, count), jnp.int32)
-    to_upper, to_lower, meta = pl.pallas_call(
+    to_mate, to_cross, meta = pl.pallas_call(
         pack_kernel,
         out_shape=(packed, packed, jax.ShapeDtypeStruct((8, BLOCK), jnp.float32)),
         in_specs=[hbm, hbm, hbm],
@@ -249,8 +270,8 @@
         pltpu.with_memory_space_constraint(array, pltpu.HBM)
         for array in (vectors, offsets.T, tile_ids.T)
     ))
-    before = lax.ppermute(to_upper, ROWS, up)
-    after = lax.ppermute(to_lower, ROWS, down)
+    cross = lax.ppermute(to_cross, ROWS, across)
+    mate = lax.ppermute(to_mate, ROWS, mates)
 
     table = pl.pallas_call(
         table_kernel,
@@ -283,7 +304,7 @@
         ],
         compiler_params=pltpu.CompilerParams(vmem_limit_bytes=16 * MIB),
         name="filter",
-    )(vectors, before, after, meta, table, bounds)
+    )(vectors, mate, cross, meta, table, bounds)
 
     stacked = lax.all_to_all(
         outgoing,

time: 72.9 us -> 73 us (level)
  blocking collectives: 51.4 us -> 49.2 us
  waiting for transfers between devices: 0.01 us -> 1.66 us
    all_to_all x1, blocking collectives: 28.6 us -> 24.5 us  [on_device(): lax.all_to_all(outgoing, VEC, split_axis=0, concat_axis=0, tiled=True, ax...]
    all_to_all x1, blocking collectives: 22.8 us -> 24.7 us  [on_device(): lax.all_to_all(partial.reshape(owned, 1, total), OWNERS, split_axis=0, co...]
    ppermute x2, waiting for transfers between devices: 0.01 us -> 1.66 us  [the longest x1 1.66 us: on_device(): cross = lax.ppermute(to_cross, ROWS, across)]
  transfers between devices with their start and end apart: 2 -> 2, of which waited for: 0 -> 1; matrix products, arithmetic and copies ran while one was open for 0% -> 0% of each run, Pallas kernels for 2% -> 2%
where the time goes in v7:
time: 73 us; the launch traced here: 72.8 us
  blocking collectives  49.2 us (67%)
  starting transfers between devices  10.7 us (15%)
  Pallas kernels  9.78 us (13%)
  waiting for transfers between devices  1.66 us (2%)
  other arithmetic  0.79 us (1%)
    all_to_all x1, blocking collectives, on_device(): lax.all_to_all(partial.reshape(owned, 1, total), OWNERS, split_axis=0, co...  24.7 us
    all_to_all x1, blocking collectives, on_device(): lax.all_to_all(outgoing, VEC, split_axis=0, concat_axis=0, tiled=True, ax...  24.5 us
    ppermute x1, starting transfers between devices, on_device(): mate = lax.ppermute(to_mate, ROWS, mates)  8.75 us
    pallas_call x1, Pallas kernels, on_device(): pl.pallas_call(filter_kernel, out_shape=(jax.ShapeDtypeStruct((vecs, loca...  6.82 us
    ppermute x1, starting transfers between devices, on_device(): cross = lax.ppermute(to_cross, ROWS, across)  1.92 us
    pallas_call x1, Pallas kernels, on_device(): pl.pallas_call(table_kernel, out_shape=jax.ShapeDtypeStruct((3 * NT, BLOC...  1.67 us
    ppermute x1, waiting for transfers between devices, on_device(): cross = lax.ppermute(to_cross, ROWS, across)  1.66 us
  transfers between devices with their start and end apart: 2, of which 1 were waited for; matrix products, arithmetic and copies ran while one was open for 0% of the time, Pallas kernels for 2%

profile of v7, /device:TPU:1, one launch (start us, length us, event | category | flops | bytes accessed | tf_op | source)
XLA Modules:
  0.0 72.8 jit_solution(13399510651323558304)
XLA Ops:
  0.6 0.0 copy-start
  0.6 0.0 copy-start.1
  0.7 0.9 %pack.1 = (f32[8,1152]{1,0:T(8,128)S(1)}, f32[8,1152]{1,0:T(8,128)S(1)}, f32[8,128]{1,0:T(8,128)S(1)}) custom-call(f32[8,4096]{1,0:T(8,128)} %vectors_ref.3, s32[3,32]{1,0:T(4,128)} %bitcast.7, s32[3,32]{1,0:T(4,128)} %bitcast.8), custom_call_target="tpu_custom_call" | custom-call | tf_op jit(solution)/shard_map/pack/pallas_call | solution.py:261
  1.6 8.7 %collective-permute-start = (f32[8,1152]{1,0:T(8,128)S(1)}, f32[8,1152]{1,0:T(8,128)S(1)}, u32[]{:S(2)}, u32[]{:S(2)}) collective-permute-start(f32[8,1152]{1,0:T(8,128)S(1)} %get-tuple-element.7), channel_id=1, source_target_pairs={{0,64},{64,0},{128,192},{192,128},{256,320},{320,256},{384,448},{4... | collective-permute-start | bytes 110600 | tf_op jit(solution)/shard_map/ppermute | solution.py:274
  10.3 1.9 %collective-permute-start.1 = (f32[8,1152]{1,0:T(8,128)S(1)}, f32[8,1152]{1,0:T(8,128)S(1)}, u32[]{:S(2)}, u32[]{:S(2)}) collective-permute-start(f32[8,1152]{1,0:T(8,128)S(1)} %get-tuple-element.8), channel_id=1, source_target_pairs={{64,128},{128,64},{192,256},{256,192},{320,384},{384,320},{65,129}... | collective-permute-start | bytes 110600 | tf_op jit(solution)/shard_map/ppermute | solution.py:273
  12.2 1.7 %table.1.table_ref = bf16[48,128,256]{2,1,0:T(8,128)(2,1)S(1)} custom-call(f32[16,128,128]{2,1,0:T(8,128)} %tiles_ref.1), custom_call_target="tpu_custom_call" | custom-call | tf_op jit(solution)/shard_map/table/pallas_call | solution.py:276
  13.9 0.0 collective-permute-done.mate_ref
  13.9 1.7 %collective-permute-done.1.cross_ref = f32[8,1152]{1,0:T(8,128)S(1)} collective-permute-done((f32[8,1152]{1,0:T(8,128)S(1)}, f32[8,1152]{1,0:T(8,128)S(1)}, u32[]{:S(2)}, u32[]{:S(2)}) %collective-permute-start.1) | collective-permute-done | bytes 36896 | tf_op jit(solution)/shard_map/ppermute | solution.py:273
  15.6 0.0 copy-done
  15.6 0.0 copy-done.1
  15.6 6.8 %filter.1 = (f32[8,4096]{1,0:T(8,128)}, f32[64,8,256]{2,1,0:T(8,128)S(1)}) custom-call(f32[8,4096]{1,0:T(8,128)S(1)} %copy-done, f32[8,1152]{1,0:T(8,128)S(1)} %collective-permute-done.mate_ref, f32[8,1152]{1,0:T(8,128)S(1)} %collective-permute-done.1.cross_ref, f32[8,128]{1,0:T(8,128)S(1)} %get-tuple-element.9.own_ref, ...), custom_call_target="tpu_custom_call" | custom-call | tf_op jit(solution)/shard_map/filter/pallas_call | solution.py:291
  22.4 24.5 %all_to_all.10 = f32[64,8,256]{2,1,0:T(8,128)S(1)} all-to-all(f32[64,8,256]{2,1,0:T(8,128)S(1)} %get-tuple-element.11), channel_id=1, replica_groups={{41,40,43,42,45,44,47,46,33,32,35,34,37,36,39,38,57,56,59,58,61,60,63,6..., dimensions={0} | all-to-all | bytes 1048576 | tf_op jit(solution)/shard_map/all_to_all | solution.py:309
  46.9 0.4 gram.1
  47.3 24.7 %all_to_all.11 = f32[128,1,512]{2,1,0:T(1,128)S(1)} all-to-all(f32[128,1,512]{2,1,0:T(1,128)S(1)} %bitcast.6), channel_id=1, replica_groups={{416,417,418,419,432,433,434,435,384,385,386,387,400,401,402,403,480,48..., dimensions={0} | all-to-all | bytes 524288 | tf_op jit(solution)/shard_map/all_to_all | solution.py:330
  72.0 0.8 %reduce_sum.11 = f32[512]{0:T(512)} reduce(f32[128,1,512]{2,1,0:T(1,128)S(1)} %all_to_all.11, f32[]{:T(128)} %constant.0.clone.1), dimensions={0,1}, to_apply=%region_0.0 | reduce | flops 65024 | bytes 264196 | tf_op jit(solution)/shard_map/reduce_sum | solution.py:338
Async XLA Ops:
  0.6 15.0 %copy-start = (f32[8,4096]{1,0:T(8,128)S(1)}, f32[8,4096]{1,0:T(8,128)}, u32[]{:S(2)}) copy-start(f32[8,4096]{1,0:T(8,128)} %vectors_ref.3) | copy-start | bytes 393220
  0.6 15.0 %copy-start.1 = (f32[3]{0:T(128)S(1)}, f32[3]{0:T(128)}, u32[]{:S(2)}) copy-start(f32[3]{0:T(128)} %bounds_ref.1) | copy-start | bytes 40
  1.6 12.4 %collective-permute-start = (f32[8,1152]{1,0:T(8,128)S(1)}, f32[8,1152]{1,0:T(8,128)S(1)}, u32[]{:S(2)}, u32[]{:S(2)}) collective-permute-start(f32[8,1152]{1,0:T(8,128)S(1)} %get-tuple-element.7), channel_id=1, source_target_pairs={{0,64},{64,0},{128,192},{192,128},{256,320},{320,256},{384,448},{4... | collective-permute-start | bytes 110600 | tf_op jit(solution)/shard_map/ppermute | solution.py:274
  10.3 5.3 %collective-permute-start.1 = (f32[8,1152]{1,0:T(8,128)S(1)}, f32[8,1152]{1,0:T(8,128)S(1)}, u32[]{:S(2)}, u32[]{:S(2)}) collective-permute-start(f32[8,1152]{1,0:T(8,128)S(1)} %get-tuple-element.8), channel_id=1, source_target_pairs={{64,128},{128,64},{192,256},{256,192},{320,384},{384,320},{65,129}... | collective-permute-start | bytes 110600 | tf_op jit(solution)/shard_map/ppermute | solution.py:273

commit v8 on v7

--- a/solution.py
+++ b/solution.py
@@ -17,7 +17,7 @@
 VEC = ("x", "yq", "yb", "zh")
 OWNERS = ROWS + ("x", "yb", "zh")
 FIRST_TURN = 0b101001
-SECOND_TURN = 0b1101000
+SECOND_TURN = 0b1101001
 
 
 def split(value):
@@ -192,7 +192,12 @@
                 one_block(first + index * group + inner, (index, inner // 2), inner % 2)
 
 
-def gram_kernel(scale, stacked_ref, partial_ref, all_high, all_low, own_high, own_low):
+def gram_kernel(
+    scale, stacked_ref, filtered_ref, partial_ref, kept_ref,
+    all_high, all_low, own_high, own_low, sem,
+):
+    keep = pltpu.make_async_copy(filtered_ref, kept_ref, sem)
+    keep.start()
     total = stacked_ref.shape[0]
     quarter = lax.axis_index("yq")
 
@@ -243,6 +248,7 @@
         partial_ref[pl.ds(piece, count, stride=pieces), :] = partial[
             :, piece * BLOCK : (piece + 1) * BLOCK
         ]
+    keep.wait()
 
 
 def on_device(vectors, tile_table, offsets, tile_ids, bounds):
@@ -291,7 +297,7 @@
     filtered, outgoing = pl.pallas_call(
         filter_kernel,
         out_shape=(
-            jax.ShapeDtypeStruct((vecs, local_rows), jnp.float32),
+            pltpu.VMEM((vecs, local_rows), jnp.float32),
             jax.ShapeDtypeStruct((64, vecs, 2 * BLOCK), jnp.float32),
         ),
         in_specs=[vmem, vmem, vmem, vmem, vmem, smem],
@@ -317,16 +323,20 @@
     total = 64 * vecs
     stacked = stacked.reshape(total, 2 * BLOCK)
     owned = total // 4
-    partial = pl.pallas_call(
+    partial, kept = pl.pallas_call(
         functools.partial(gram_kernel, 1.0 / (local_rows * size)),
-        out_shape=jax.ShapeDtypeStruct((owned * (total // BLOCK), BLOCK), jnp.float32),
-        in_specs=[vmem],
-        out_specs=vmem,
+        out_shape=(
+            jax.ShapeDtypeStruct((owned * (total // BLOCK), BLOCK), jnp.float32),
+            jax.ShapeDtypeStruct(filtered.shape, jnp.float32),
+        ),
+        in_specs=[vmem, vmem],
+        out_specs=(vmem, hbm),
         scratch_shapes=[pltpu.VMEM((total, 2 * BLOCK), jnp.bfloat16)] * 2
-        + [pltpu.VMEM((owned, 2 * BLOCK), jnp.bfloat16)] * 2,
+        + [pltpu.VMEM((owned, 2 * BLOCK), jnp.bfloat16)] * 2
+        + [pltpu.SemaphoreType.DMA(())],
         compiler_params=pltpu.CompilerParams(vmem_limit_bytes=16 * MIB),
         name="gram",
-    )(stacked)
+    )(stacked, filtered)
     received = lax.all_to_all(
         partial.reshape(owned, 1, total),
         OWNERS,
@@ -336,7 +346,7 @@
         axis_index_groups=[[at ^ SECOND_TURN for at in range(owned)]],
     )
     gram_matrix = jnp.sum(received, axis=0)
-    return filtered, gram_matrix
+    return kept, gram_matrix
 
 
 def solution(mesh):

time: 73 us -> 70.6 us (0.967)
  blocking collectives: 49.2 us -> 47.1 us
    all_to_all x1, blocking collectives: 24.7 us -> 22.6 us  [on_device(): lax.all_to_all(partial.reshape(owned, 1, total), OWNERS, split_axis=0, co...]
where the time goes in v8:
time: 70.6 us; the launch traced here: 70.4 us
  blocking collectives  47.1 us (67%)
  starting transfers between devices  10.7 us (15%)
  Pallas kernels  9.48 us (13%)
  waiting for transfers between devices  1.66 us (2%)
  other arithmetic  0.79 us (1%)
    all_to_all x1, blocking collectives, on_device(): lax.all_to_all(outgoing, VEC, split_axis=0, concat_axis=0, tiled=True, ax...  24.5 us
    all_to_all x1, blocking collectives, on_device(): lax.all_to_all(partial.reshape(owned, 1, total), OWNERS, split_axis=0, co...  22.6 us
    ppermute x1, starting transfers between devices, on_device(): mate = lax.ppermute(to_mate, ROWS, mates)  8.75 us
    pallas_call x1, Pallas kernels, on_device(): pl.pallas_call(filter_kernel, out_shape=(pltpu.VMEM((vecs, local_rows), j...  6.17 us
    ppermute x1, starting transfers between devices, on_device(): cross = lax.ppermute(to_cross, ROWS, across)  1.92 us
    pallas_call x1, Pallas kernels, on_device(): pl.pallas_call(table_kernel, out_shape=jax.ShapeDtypeStruct((3 * NT, BLOC...  1.67 us
    ppermute x1, waiting for transfers between devices, on_device(): cross = lax.ppermute(to_cross, ROWS, across)  1.66 us
  transfers between devices with their start and end apart: 2, of which 1 were waited for; matrix products, arithmetic and copies ran while one was open for 0% of the time, Pallas kernels for 2%

profile of v8, /device:TPU:1, one launch (start us, length us, event | category | flops | bytes accessed | tf_op | source)
XLA Modules:
  0.0 70.4 jit_solution(11578805289946516036)
XLA Ops:
  0.6 0.0 copy-start
  0.6 0.0 copy-start.1
  0.7 0.9 %pack.1 = (f32[8,1152]{1,0:T(8,128)S(1)}, f32[8,1152]{1,0:T(8,128)S(1)}, f32[8,128]{1,0:T(8,128)S(1)}) custom-call(f32[8,4096]{1,0:T(8,128)} %vectors_ref.3, s32[3,32]{1,0:T(4,128)} %bitcast.7, s32[3,32]{1,0:T(4,128)} %bitcast.8), custom_call_target="tpu_custom_call" | custom-call | tf_op jit(solution)/shard_map/pack/pallas_call | solution.py:267
  1.6 8.7 %collective-permute-start = (f32[8,1152]{1,0:T(8,128)S(1)}, f32[8,1152]{1,0:T(8,128)S(1)}, u32[]{:S(2)}, u32[]{:S(2)}) collective-permute-start(f32[8,1152]{1,0:T(8,128)S(1)} %get-tuple-element.9), channel_id=1, source_target_pairs={{0,64},{64,0},{128,192},{192,128},{256,320},{320,256},{384,448},{4... | collective-permute-start | bytes 110600 | tf_op jit(solution)/shard_map/ppermute | solution.py:280
  10.3 1.9 %collective-permute-start.1 = (f32[8,1152]{1,0:T(8,128)S(1)}, f32[8,1152]{1,0:T(8,128)S(1)}, u32[]{:S(2)}, u32[]{:S(2)}) collective-permute-start(f32[8,1152]{1,0:T(8,128)S(1)} %get-tuple-element.10), channel_id=1, source_target_pairs={{64,128},{128,64},{192,256},{256,192},{320,384},{384,320},{65,129}... | collective-permute-start | bytes 110600 | tf_op jit(solution)/shard_map/ppermute | solution.py:279
  12.2 1.7 %table.1.table_ref = bf16[48,128,256]{2,1,0:T(8,128)(2,1)S(1)} custom-call(f32[16,128,128]{2,1,0:T(8,128)} %tiles_ref.1), custom_call_target="tpu_custom_call" | custom-call | tf_op jit(solution)/shard_map/table/pallas_call | solution.py:282
  13.9 0.0 collective-permute-done.mate_ref
  13.9 1.7 %collective-permute-done.1.cross_ref = f32[8,1152]{1,0:T(8,128)S(1)} collective-permute-done((f32[8,1152]{1,0:T(8,128)S(1)}, f32[8,1152]{1,0:T(8,128)S(1)}, u32[]{:S(2)}, u32[]{:S(2)}) %collective-permute-start.1) | collective-permute-done | bytes 36896 | tf_op jit(solution)/shard_map/ppermute | solution.py:279
  15.6 0.0 copy-done
  15.6 0.0 copy-done.1
  15.6 6.2 %filter.1 = (f32[8,4096]{1,0:T(8,128)S(1)}, f32[64,8,256]{2,1,0:T(8,128)S(1)}) custom-call(f32[8,4096]{1,0:T(8,128)S(1)} %copy-done, f32[8,1152]{1,0:T(8,128)S(1)} %collective-permute-done.mate_ref, f32[8,1152]{1,0:T(8,128)S(1)} %collective-permute-done.1.cross_ref, f32[8,128]{1,0:T(8,128)S(1)} %get-tuple-element.11.own_ref, ...), custom_call_target="tpu_custom_call" | custom-call | tf_op jit(solution)/shard_map/filter/pallas_call | solution.py:297
  21.8 24.5 %all_to_all.10 = f32[64,8,256]{2,1,0:T(8,128)S(1)} all-to-all(f32[64,8,256]{2,1,0:T(8,128)S(1)} %get-tuple-element.12), channel_id=1, replica_groups={{41,40,43,42,45,44,47,46,33,32,35,34,37,36,39,38,57,56,59,58,61,60,63,6..., dimensions={0} | all-to-all | bytes 1048576 | tf_op jit(solution)/shard_map/all_to_all | solution.py:315
  46.2 0.7 %gram.1 = (f32[512,128]{1,0:T(8,128)S(1)}, f32[8,4096]{1,0:T(8,128)}) custom-call(f32[512,256]{1,0:T(8,128)S(1)} %bitcast.5, f32[8,4096]{1,0:T(8,128)S(1)} %get-tuple-element.13.filtered_ref), custom_call_target="tpu_custom_call" | custom-call | tf_op jit(solution)/shard_map/gram/pallas_call | solution.py:326
  47.0 22.6 %all_to_all.11 = f32[128,1,512]{2,1,0:T(1,128)S(1)} all-to-all(f32[128,1,512]{2,1,0:T(1,128)S(1)} %bitcast.6), channel_id=1, replica_groups={{417,416,419,418,433,432,435,434,385,384,387,386,401,400,403,402,481,48..., dimensions={0} | all-to-all | bytes 524288 | tf_op jit(solution)/shard_map/all_to_all | solution.py:340
  69.6 0.8 %reduce_sum.11 = f32[512]{0:T(512)} reduce(f32[128,1,512]{2,1,0:T(1,128)S(1)} %all_to_all.11, f32[]{:T(128)} %constant.0.clone.1), dimensions={0,1}, to_apply=%region_0.0 | reduce | flops 65024 | bytes 264196 | tf_op jit(solution)/shard_map/reduce_sum | solution.py:348
Async XLA Ops:
  0.6 15.0 %copy-start = (f32[8,4096]{1,0:T(8,128)S(1)}, f32[8,4096]{1,0:T(8,128)}, u32[]{:S(2)}) copy-start(f32[8,4096]{1,0:T(8,128)} %vectors_ref.3) | copy-start | bytes 393220
  0.6 15.0 %copy-start.1 = (f32[3]{0:T(128)S(1)}, f32[3]{0:T(128)}, u32[]{:S(2)}) copy-start(f32[3]{0:T(128)} %bounds_ref.1) | copy-start | bytes 40
  1.6 12.4 %collective-permute-start = (f32[8,1152]{1,0:T(8,128)S(1)}, f32[8,1152]{1,0:T(8,128)S(1)}, u32[]{:S(2)}, u32[]{:S(2)}) collective-permute-start(f32[8,1152]{1,0:T(8,128)S(1)} %get-tuple-element.9), channel_id=1, source_target_pairs={{0,64},{64,0},{128,192},{192,128},{256,320},{320,256},{384,448},{4... | collective-permute-start | bytes 110600 | tf_op jit(solution)/shard_map/ppermute | solution.py:280
  10.3 5.3 %collective-permute-start.1 = (f32[8,1152]{1,0:T(8,128)S(1)}, f32[8,1152]{1,0:T(8,128)S(1)}, u32[]{:S(2)}, u32[]{:S(2)}) collective-permute-start(f32[8,1152]{1,0:T(8,128)S(1)} %get-tuple-element.10), channel_id=1, source_target_pairs={{64,128},{128,64},{192,256},{256,192},{320,384},{384,320},{65,129}... | collective-permute-start | bytes 110600 | tf_op jit(solution)/shard_map/ppermute | solution.py:279

commit v9 on v8

--- a/solution.py
+++ b/solution.py
@@ -16,8 +16,8 @@
 ROWS = ("zl", "core")
 VEC = ("x", "yq", "yb", "zh")
 OWNERS = ROWS + ("x", "yb", "zh")
-FIRST_TURN = 0b101001
-SECOND_TURN = 0b1101001
+FIRST_TURN = 0b101011
+SECOND_TURN = 0b1111001
 
 
 def split(value):
@@ -249,6 +249,15 @@
             :, piece * BLOCK : (piece + 1) * BLOCK
         ]
     keep.wait()
+
+
+def sum_kernel(received_ref, row_ref):
+    tiles = received_ref.shape[0] // 8
+    sums = [received_ref[at * 8 : (at + 1) * 8, :] for at in range(4)]
+    for at in range(4, tiles):
+        sums[at % 4] = sums[at % 4] + received_ref[at * 8 : (at + 1) * 8, :]
+    total = (sums[0] + sums[1]) + (sums[2] + sums[3])
+    row_ref[...] = total[:4, :] + total[4:, :]
 
 
 def on_device(vectors, tile_table, offsets, tile_ids, bounds):
@@ -345,7 +354,14 @@
         tiled=True,
         axis_index_groups=[[at ^ SECOND_TURN for at in range(owned)]],
     )
-    gram_matrix = jnp.sum(received, axis=0)
+    gram_matrix = pl.pallas_call(
+        sum_kernel,
+        out_shape=jax.ShapeDtypeStruct((total // BLOCK, BLOCK), jnp.float32),
+        in_specs=[vmem],
+        out_specs=vmem,
+        compiler_params=pltpu.CompilerParams(vmem_limit_bytes=4 * MIB),
+        name="sum",
+    )(received.reshape(owned * (total // BLOCK), BLOCK)).reshape(1, total)
     return kept, gram_matrix
 
 

time: 70.6 us -> 70 us (level)
  other arithmetic: 0.79 us -> 0 us
    reduce_sum x1 -> x0, other arithmetic: 0.79 us -> none  [on_device(): gram_matrix = jnp.sum(received, axis=0)]
where the time goes in v9:
time: 70 us; the launch traced here: 69.8 us
  blocking collectives  46.7 us (67%)
  starting transfers between devices  10.7 us (15%)
  Pallas kernels  10.1 us (14%)
  waiting for transfers between devices  1.66 us (2%)
    all_to_all x1, blocking collectives, on_device(): lax.all_to_all(outgoing, VEC, split_axis=0, concat_axis=0, tiled=True, ax...  24.6 us
    all_to_all x1, blocking collectives, on_device(): lax.all_to_all(partial.reshape(owned, 1, total), OWNERS, split_axis=0, co...  22.1 us
    ppermute x1, starting transfers between devices, on_device(): mate = lax.ppermute(to_mate, ROWS, mates)  8.75 us
    pallas_call x1, Pallas kernels, on_device(): pl.pallas_call(filter_kernel, out_shape=(pltpu.VMEM((vecs, local_rows), j...  6.17 us
    ppermute x1, starting transfers between devices, on_device(): cross = lax.ppermute(to_cross, ROWS, across)  1.92 us
    pallas_call x1, Pallas kernels, on_device(): pl.pallas_call(table_kernel, out_shape=jax.ShapeDtypeStruct((3 * NT, BLOC...  1.67 us
    ppermute x1, waiting for transfers between devices, on_device(): cross = lax.ppermute(to_cross, ROWS, across)  1.66 us
  transfers between devices with their start and end apart: 2, of which 1 were waited for; matrix products, arithmetic and copies ran while one was open for 0% of the time, Pallas kernels for 2%

profile of v9, /device:TPU:1, one launch (start us, length us, event | category | flops | bytes accessed | tf_op | source)
XLA Modules:
  0.0 69.8 jit_solution(11825416585815186212)
XLA Ops:
  0.6 0.0 copy-start
  0.6 0.0 copy-start.1
  0.7 0.9 %pack.1 = (f32[8,1152]{1,0:T(8,128)S(1)}, f32[8,1152]{1,0:T(8,128)S(1)}, f32[8,128]{1,0:T(8,128)S(1)}) custom-call(f32[8,4096]{1,0:T(8,128)} %vectors_ref.3, s32[3,32]{1,0:T(4,128)} %bitcast.9, s32[3,32]{1,0:T(4,128)} %bitcast.10), custom_call_target="tpu_custom_call" | custom-call | tf_op jit(solution)/shard_map/pack/pallas_call | solution.py:276
  1.6 8.7 %collective-permute-start = (f32[8,1152]{1,0:T(8,128)S(1)}, f32[8,1152]{1,0:T(8,128)S(1)}, u32[]{:S(2)}, u32[]{:S(2)}) collective-permute-start(f32[8,1152]{1,0:T(8,128)S(1)} %get-tuple-element.9), channel_id=1, source_target_pairs={{0,64},{64,0},{128,192},{192,128},{256,320},{320,256},{384,448},{4... | collective-permute-start | bytes 110600 | tf_op jit(solution)/shard_map/ppermute | solution.py:289
  10.3 1.9 %collective-permute-start.1 = (f32[8,1152]{1,0:T(8,128)S(1)}, f32[8,1152]{1,0:T(8,128)S(1)}, u32[]{:S(2)}, u32[]{:S(2)}) collective-permute-start(f32[8,1152]{1,0:T(8,128)S(1)} %get-tuple-element.10), channel_id=1, source_target_pairs={{64,128},{128,64},{192,256},{256,192},{320,384},{384,320},{65,129}... | collective-permute-start | bytes 110600 | tf_op jit(solution)/shard_map/ppermute | solution.py:288
  12.2 1.7 %table.1.table_ref = bf16[48,128,256]{2,1,0:T(8,128)(2,1)S(1)} custom-call(f32[16,128,128]{2,1,0:T(8,128)} %tiles_ref.1), custom_call_target="tpu_custom_call" | custom-call | tf_op jit(solution)/shard_map/table/pallas_call | solution.py:291
  13.9 0.0 collective-permute-done.mate_ref
  13.9 1.7 %collective-permute-done.1.cross_ref = f32[8,1152]{1,0:T(8,128)S(1)} collective-permute-done((f32[8,1152]{1,0:T(8,128)S(1)}, f32[8,1152]{1,0:T(8,128)S(1)}, u32[]{:S(2)}, u32[]{:S(2)}) %collective-permute-start.1) | collective-permute-done | bytes 36896 | tf_op jit(solution)/shard_map/ppermute | solution.py:288
  15.6 0.0 copy-done
  15.6 0.0 copy-done.1
  15.6 6.2 %filter.1 = (f32[8,4096]{1,0:T(8,128)S(1)}, f32[64,8,256]{2,1,0:T(8,128)S(1)}) custom-call(f32[8,4096]{1,0:T(8,128)S(1)} %copy-done, f32[8,1152]{1,0:T(8,128)S(1)} %collective-permute-done.mate_ref, f32[8,1152]{1,0:T(8,128)S(1)} %collective-permute-done.1.cross_ref, f32[8,128]{1,0:T(8,128)S(1)} %get-tuple-element.11.own_ref, ...), custom_call_target="tpu_custom_call" | custom-call | tf_op jit(solution)/shard_map/filter/pallas_call | solution.py:306
  21.8 24.6 %all_to_all.10 = f32[64,8,256]{2,1,0:T(8,128)S(1)} all-to-all(f32[64,8,256]{2,1,0:T(8,128)S(1)} %get-tuple-element.12), channel_id=1, replica_groups={{43,42,41,40,47,46,45,44,35,34,33,32,39,38,37,36,59,58,57,56,63,62,61,6..., dimensions={0} | all-to-all | bytes 1048576 | tf_op jit(solution)/shard_map/all_to_all | solution.py:324
  46.4 0.7 %gram.1 = (f32[512,128]{1,0:T(8,128)S(1)}, f32[8,4096]{1,0:T(8,128)}) custom-call(f32[512,256]{1,0:T(8,128)S(1)} %bitcast.6, f32[8,4096]{1,0:T(8,128)S(1)} %get-tuple-element.13.filtered_ref), custom_call_target="tpu_custom_call" | custom-call | tf_op jit(solution)/shard_map/gram/pallas_call | solution.py:335
  47.1 22.1 %all_to_all.11 = f32[128,1,512]{2,1,0:T(1,128)S(1)} all-to-all(f32[128,1,512]{2,1,0:T(1,128)S(1)} %bitcast.8), channel_id=1, replica_groups={{481,480,483,482,497,496,499,498,449,448,451,450,465,464,467,466,417,41..., dimensions={0} | all-to-all | bytes 524288 | tf_op jit(solution)/shard_map/all_to_all | solution.py:349
  69.2 0.6 sum.1
Async XLA Ops:
  0.6 15.0 %copy-start = (f32[8,4096]{1,0:T(8,128)S(1)}, f32[8,4096]{1,0:T(8,128)}, u32[]{:S(2)}) copy-start(f32[8,4096]{1,0:T(8,128)} %vectors_ref.3) | copy-start | bytes 393220
  0.6 15.0 %copy-start.1 = (f32[3]{0:T(128)S(1)}, f32[3]{0:T(128)}, u32[]{:S(2)}) copy-start(f32[3]{0:T(128)} %bounds_ref.1) | copy-start | bytes 40
  1.6 12.4 %collective-permute-start = (f32[8,1152]{1,0:T(8,128)S(1)}, f32[8,1152]{1,0:T(8,128)S(1)}, u32[]{:S(2)}, u32[]{:S(2)}) collective-permute-start(f32[8,1152]{1,0:T(8,128)S(1)} %get-tuple-element.9), channel_id=1, source_target_pairs={{0,64},{64,0},{128,192},{192,128},{256,320},{320,256},{384,448},{4... | collective-permute-start | bytes 110600 | tf_op jit(solution)/shard_map/ppermute | solution.py:289
  10.3 5.3 %collective-permute-start.1 = (f32[8,1152]{1,0:T(8,128)S(1)}, f32[8,1152]{1,0:T(8,128)S(1)}, u32[]{:S(2)}, u32[]{:S(2)}) collective-permute-start(f32[8,1152]{1,0:T(8,128)S(1)} %get-tuple-element.10), channel_id=1, source_target_pairs={{64,128},{128,64},{192,256},{256,192},{320,384},{384,320},{65,129}... | collective-permute-start | bytes 110600 | tf_op jit(solution)/shard_map/ppermute | solution.py:288

commit v10 on v7

--- a/solution.py
+++ b/solution.py
@@ -6,6 +6,7 @@
 from jax.experimental import pallas as pl
 from jax.experimental.pallas import tpu as pltpu
 from jax.sharding import Mesh, PartitionSpec as P
+
 
 BLOCK = 128
 STEPS = 4
@@ -16,8 +17,8 @@
 ROWS = ("zl", "core")
 VEC = ("x", "yq", "yb", "zh")
 OWNERS = ROWS + ("x", "yb", "zh")
-FIRST_TURN = 0b101001
-SECOND_TURN = 0b1101000
+FIRST_TURN = 0b101011
+SECOND_TURN = 0b1111001
 
 
 def split(value):
@@ -192,7 +193,9 @@
                 one_block(first + index * group + inner, (index, inner // 2), inner % 2)
 
 
-def gram_kernel(scale, stacked_ref, partial_ref, all_high, all_low, own_high, own_low):
+def gram_kernel(
+    scale, stacked_ref, partial_ref, all_high, all_low, own_high, own_low
+):
     total = stacked_ref.shape[0]
     quarter = lax.axis_index("yq")
 
@@ -243,6 +246,18 @@
         partial_ref[pl.ds(piece, count, stride=pieces), :] = partial[
             :, piece * BLOCK : (piece + 1) * BLOCK
         ]
+
+
+def sum_kernel(received_ref, filtered_ref, row_ref, kept_ref, sem):
+    keep = pltpu.make_async_copy(filtered_ref, kept_ref, sem)
+    keep.start()
+    tiles = received_ref.shape[0] // 8
+    sums = [received_ref[at * 8 : (at + 1) * 8, :] for at in range(4)]
+    for at in range(4, tiles):
+        sums[at % 4] = sums[at % 4] + received_ref[at * 8 : (at + 1) * 8, :]
+    total = (sums[0] + sums[1]) + (sums[2] + sums[3])
+    row_ref[...] = total[:4, :] + total[4:, :]
+    keep.wait()
 
 
 def on_device(vectors, tile_table, offsets, tile_ids, bounds):
@@ -280,7 +295,7 @@
         out_specs=vmem,
         scratch_shapes=[
             pltpu.VMEM(tile_table.shape, jnp.float32),
-            pltpu.SemaphoreType.DMA((4,)),
+            pltpu.SemaphoreType.DMA((NT,)),
         ],
         compiler_params=pltpu.CompilerParams(vmem_limit_bytes=16 * MIB),
         name="table",
@@ -291,7 +306,7 @@
     filtered, outgoing = pl.pallas_call(
         filter_kernel,
         out_shape=(
-            jax.ShapeDtypeStruct((vecs, local_rows), jnp.float32),
+            pltpu.VMEM((vecs, local_rows), jnp.float32),
             jax.ShapeDtypeStruct((64, vecs, 2 * BLOCK), jnp.float32),
         ),
         in_specs=[vmem, vmem, vmem, vmem, vmem, smem],
@@ -335,8 +350,19 @@
         tiled=True,
         axis_index_groups=[[at ^ SECOND_TURN for at in range(owned)]],
     )
-    gram_matrix = jnp.sum(received, axis=0)
-    return filtered, gram_matrix
+    row, kept = pl.pallas_call(
+        sum_kernel,
+        out_shape=(
+            jax.ShapeDtypeStruct((total // BLOCK, BLOCK), jnp.float32),
+            jax.ShapeDtypeStruct(filtered.shape, jnp.float32),
+        ),
+        in_specs=[vmem, vmem],
+        out_specs=(vmem, hbm),
+        scratch_shapes=[pltpu.SemaphoreType.DMA(())],
+        compiler_params=pltpu.CompilerParams(vmem_limit_bytes=4 * MIB),
+        name="sum",
+    )(received.reshape(owned * (total // BLOCK), BLOCK), filtered)
+    return kept, row.reshape(1, total)
 
 
 def solution(mesh):

time: 73 us -> 70.9 us (0.971)
  blocking collectives: 49.2 us -> 47.2 us
  Pallas kernels: 9.78 us -> 11.4 us
  waiting for transfers between devices: 1.66 us -> 0.62 us
  other arithmetic: 0.79 us -> 0 us
    all_to_all x1, blocking collectives: 24.7 us -> 21.6 us  [on_device(): lax.all_to_all(partial.reshape(owned, 1, total), OWNERS, split_axis=0, co...]
    all_to_all x1, blocking collectives: 24.5 us -> 25.6 us  [on_device(): lax.all_to_all(outgoing, VEC, split_axis=0, concat_axis=0, tiled=True, ax...]
    pallas_call x1, Pallas kernels: 1.67 us -> 2.71 us  [on_device(): pl.pallas_call(table_kernel, out_shape=jax.ShapeDtypeStruct((3 * NT, BLOC...]
    ppermute x1, waiting for transfers between devices: 1.66 us -> 0.62 us  [on_device(): cross = lax.ppermute(to_cross, ROWS, across)]
    reduce_sum x1 -> x0, other arithmetic: 0.79 us -> none  [on_device(): gram_matrix = jnp.sum(received, axis=0)]
    pallas_call x1 -> x2, Pallas kernels: 6.82 us -> 7.41 us  [the longest x1 6.17 us: on_device(): pl.pallas_call(filter_kernel, out_shape=(pltpu.VMEM((vecs, local_rows), j...]
  transfers between devices with their start and end apart: 2 -> 2, of which waited for: 1 -> 1; matrix products, arithmetic and copies ran while one was open for 0% -> 0% of each run, Pallas kernels for 2% -> 4%
where the time goes in v10:
time: 70.9 us; the launch traced here: 70.6 us
  blocking collectives  47.2 us (67%)
  Pallas kernels  11.4 us (16%)
  starting transfers between devices  10.7 us (15%)
    all_to_all x1, blocking collectives, on_device(): lax.all_to_all(outgoing, VEC, split_axis=0, concat_axis=0, tiled=True, ax...  25.6 us
    all_to_all x1, blocking collectives, on_device(): lax.all_to_all(partial.reshape(owned, 1, total), OWNERS, split_axis=0, co...  21.6 us
    ppermute x1, starting transfers between devices, on_device(): mate = lax.ppermute(to_mate, ROWS, mates)  8.75 us
    pallas_call x1, Pallas kernels, on_device(): pl.pallas_call(filter_kernel, out_shape=(pltpu.VMEM((vecs, local_rows), j...  6.17 us
    pallas_call x1, Pallas kernels, on_device(): pl.pallas_call(table_kernel, out_shape=jax.ShapeDtypeStruct((3 * NT, BLOC...  2.71 us
    ppermute x1, starting transfers between devices, on_device(): cross = lax.ppermute(to_cross, ROWS, across)  1.92 us
  transfers between devices with their start and end apart: 2, of which 1 were waited for; matrix products, arithmetic and copies ran while one was open for 0% of the time, Pallas kernels for 4%

profile of v10, /device:TPU:1, one launch (start us, length us, event | category | flops | bytes accessed | tf_op | source)
XLA Modules:
  0.0 70.6 jit_solution(14159858427315256664)
XLA Ops:
  0.6 0.0 copy-start
  0.6 0.0 copy-start.1
  0.7 0.9 %pack.1 = (f32[8,1152]{1,0:T(8,128)S(1)}, f32[8,1152]{1,0:T(8,128)S(1)}, f32[8,128]{1,0:T(8,128)S(1)}) custom-call(f32[8,4096]{1,0:T(8,128)} %vectors_ref.3, s32[3,32]{1,0:T(4,128)} %bitcast.9, s32[3,32]{1,0:T(4,128)} %bitcast.10), custom_call_target="tpu_custom_call" | custom-call | tf_op jit(solution)/shard_map/pack/pallas_call | solution.py:276
  1.6 8.7 %collective-permute-start = (f32[8,1152]{1,0:T(8,128)S(1)}, f32[8,1152]{1,0:T(8,128)S(1)}, u32[]{:S(2)}, u32[]{:S(2)}) collective-permute-start(f32[8,1152]{1,0:T(8,128)S(1)} %get-tuple-element.9), channel_id=1, source_target_pairs={{0,64},{64,0},{128,192},{192,128},{256,320},{320,256},{384,448},{4... | collective-permute-start | bytes 110600 | tf_op jit(solution)/shard_map/ppermute | solution.py:289
  10.3 1.9 %collective-permute-start.1 = (f32[8,1152]{1,0:T(8,128)S(1)}, f32[8,1152]{1,0:T(8,128)S(1)}, u32[]{:S(2)}, u32[]{:S(2)}) collective-permute-start(f32[8,1152]{1,0:T(8,128)S(1)} %get-tuple-element.10), channel_id=1, source_target_pairs={{64,128},{128,64},{192,256},{256,192},{320,384},{384,320},{65,129}... | collective-permute-start | bytes 110600 | tf_op jit(solution)/shard_map/ppermute | solution.py:288
  12.2 2.7 %table.1.table_ref = bf16[48,128,256]{2,1,0:T(8,128)(2,1)S(1)} custom-call(f32[16,128,128]{2,1,0:T(8,128)} %tiles_ref.1), custom_call_target="tpu_custom_call" | custom-call | tf_op jit(solution)/shard_map/table/pallas_call | solution.py:291
  15.0 0.0 collective-permute-done.mate_ref
  15.0 0.6 collective-permute-done.1.cross_ref
  15.6 0.0 copy-done
  15.6 0.0 copy-done.1
  15.6 6.2 %filter.1 = (f32[8,4096]{1,0:T(8,128)S(1)}, f32[64,8,256]{2,1,0:T(8,128)S(1)}) custom-call(f32[8,4096]{1,0:T(8,128)S(1)} %copy-done, f32[8,1152]{1,0:T(8,128)S(1)} %collective-permute-done.mate_ref, f32[8,1152]{1,0:T(8,128)S(1)} %collective-permute-done.1.cross_ref, f32[8,128]{1,0:T(8,128)S(1)} %get-tuple-element.11.own_ref, ...), custom_call_target="tpu_custom_call" | custom-call | tf_op jit(solution)/shard_map/filter/pallas_call | solution.py:306
  21.8 25.6 %all_to_all.10 = f32[64,8,256]{2,1,0:T(8,128)S(1)} all-to-all(f32[64,8,256]{2,1,0:T(8,128)S(1)} %get-tuple-element.12), channel_id=1, replica_groups={{43,42,41,40,47,46,45,44,35,34,33,32,39,38,37,36,59,58,57,56,63,62,61,6..., dimensions={0} | all-to-all | bytes 1048576 | tf_op jit(solution)/shard_map/all_to_all | solution.py:324
  47.4 0.4 gram.1
  47.8 21.6 %all_to_all.11 = f32[128,1,512]{2,1,0:T(1,128)S(1)} all-to-all(f32[128,1,512]{2,1,0:T(1,128)S(1)} %bitcast.7), channel_id=1, replica_groups={{481,480,483,482,497,496,499,498,449,448,451,450,465,464,467,466,417,41..., dimensions={0} | all-to-all | bytes 524288 | tf_op jit(solution)/shard_map/all_to_all | solution.py:345
  69.4 1.2 %sum.1 = (f32[4,128]{1,0:T(4,128)}, f32[8,4096]{1,0:T(8,128)}) custom-call(f32[512,128]{1,0:T(8,128)S(1)} %bitcast.8, f32[8,4096]{1,0:T(8,128)S(1)} %get-tuple-element.13.filtered_ref), custom_call_target="tpu_custom_call" | custom-call | tf_op jit(solution)/shard_map/sum/pallas_call | solution.py:353
Async XLA Ops:
  0.6 15.0 %copy-start = (f32[8,4096]{1,0:T(8,128)S(1)}, f32[8,4096]{1,0:T(8,128)}, u32[]{:S(2)}) copy-start(f32[8,4096]{1,0:T(8,128)} %vectors_ref.3) | copy-start | bytes 393220
  0.6 15.0 %copy-start.1 = (f32[3]{0:T(128)S(1)}, f32[3]{0:T(128)}, u32[]{:S(2)}) copy-start(f32[3]{0:T(128)} %bounds_ref.1) | copy-start | bytes 40
  1.6 13.4 %collective-permute-start = (f32[8,1152]{1,0:T(8,128)S(1)}, f32[8,1152]{1,0:T(8,128)S(1)}, u32[]{:S(2)}, u32[]{:S(2)}) collective-permute-start(f32[8,1152]{1,0:T(8,128)S(1)} %get-tuple-element.9), channel_id=1, source_target_pairs={{0,64},{64,0},{128,192},{192,128},{256,320},{320,256},{384,448},{4... | collective-permute-start | bytes 110600 | tf_op jit(solution)/shard_map/ppermute | solution.py:289
  10.3 5.3 %collective-permute-start.1 = (f32[8,1152]{1,0:T(8,128)S(1)}, f32[8,1152]{1,0:T(8,128)S(1)}, u32[]{:S(2)}, u32[]{:S(2)}) collective-permute-start(f32[8,1152]{1,0:T(8,128)S(1)} %get-tuple-element.10), channel_id=1, source_target_pairs={{64,128},{128,64},{192,256},{256,192},{320,384},{384,320},{65,129}... | collective-permute-start | bytes 110600 | tf_op jit(solution)/shard_map/ppermute | solution.py:288

commit v11 on v9

--- a/solution.py
+++ b/solution.py
@@ -6,6 +6,7 @@
 from jax.experimental import pallas as pl
 from jax.experimental.pallas import tpu as pltpu
 from jax.sharding import Mesh, PartitionSpec as P
+
 
 BLOCK = 128
 STEPS = 4
@@ -17,7 +18,7 @@
 VEC = ("x", "yq", "yb", "zh")
 OWNERS = ROWS + ("x", "yb", "zh")
 FIRST_TURN = 0b101011
-SECOND_TURN = 0b1111001
+SECOND_TURN = 0b0111001
 
 
 def split(value):
@@ -174,7 +175,7 @@
                 store_parts(parts[step], block, value)
             else:
                 at = block - HALO
-                filtered_ref[:, pl.ds(pl.multiple_of(at * BLOCK, BLOCK), BLOCK)] = value
+                filtered_ref[:, at * BLOCK : (at + 1) * BLOCK] = value
                 upper, lower = owner
                 for quarter in range(4):
                     inner = (lower // 4 * 16 + quarter * 4 + lower % 4) ^ (FIRST_TURN % 32)
@@ -184,12 +185,8 @@
                         part * BLOCK : (part + 1) * BLOCK,
                     ] = value
 
-        group = (extent - 2 * first) // 2
-
-        @pl.loop(0, 2)
-        def _(index):
-            for inner in range(group):
-                one_block(first + index * group + inner, (index, inner // 2), inner % 2)
+        for inner in range(extent - 2 * first):
+            one_block(first + inner, divmod(inner // 2, count // 4), inner % 2)
 
 
 def gram_kernel(

time: 70 us -> 69.2 us (0.989)
  no operation moved by 1% of the time
where the time goes in v11:
time: 69.2 us; the launch traced here: 68.9 us
  blocking collectives  46.4 us (67%)
  starting transfers between devices  10.7 us (15%)
  Pallas kernels  9.52 us (14%)
  waiting for transfers between devices  1.66 us (2%)
  between operations  0.7 us (1%)
    all_to_all x1, blocking collectives, on_device(): lax.all_to_all(outgoing, VEC, split_axis=0, concat_axis=0, tiled=True, ax...  24.6 us
    all_to_all x1, blocking collectives, on_device(): lax.all_to_all(partial.reshape(owned, 1, total), OWNERS, split_axis=0, co...  21.8 us
    ppermute x1, starting transfers between devices, on_device(): mate = lax.ppermute(to_mate, ROWS, mates)  8.75 us
    pallas_call x1, Pallas kernels, on_device(): pl.pallas_call(filter_kernel, out_shape=(pltpu.VMEM((vecs, local_rows), j...  5.61 us
    ppermute x1, starting transfers between devices, on_device(): cross = lax.ppermute(to_cross, ROWS, across)  1.92 us
    pallas_call x1, Pallas kernels, on_device(): pl.pallas_call(table_kernel, out_shape=jax.ShapeDtypeStruct((3 * NT, BLOC...  1.67 us
    ppermute x1, waiting for transfers between devices, on_device(): cross = lax.ppermute(to_cross, ROWS, across)  1.66 us
  transfers between devices with their start and end apart: 2, of which 1 were waited for; matrix products, arithmetic and copies ran while one was open for 0% of the time, Pallas kernels for 2%

profile of v11, /device:TPU:1, one launch (start us, length us, event | category | flops | bytes accessed | tf_op | source)
XLA Modules:
  0.0 68.9 jit_solution(9164307360153500213)
XLA Ops:
  0.6 0.0 copy-start
  0.6 0.0 copy-start.1
  0.7 0.9 %pack.1 = (f32[8,1152]{1,0:T(8,128)S(1)}, f32[8,1152]{1,0:T(8,128)S(1)}, f32[8,128]{1,0:T(8,128)S(1)}) custom-call(f32[8,4096]{1,0:T(8,128)} %vectors_ref.3, s32[3,32]{1,0:T(4,128)} %bitcast.9, s32[3,32]{1,0:T(4,128)} %bitcast.10), custom_call_target="tpu_custom_call" | custom-call | tf_op jit(solution)/shard_map/pack/pallas_call | solution.py:273
  1.6 8.7 %collective-permute-start = (f32[8,1152]{1,0:T(8,128)S(1)}, f32[8,1152]{1,0:T(8,128)S(1)}, u32[]{:S(2)}, u32[]{:S(2)}) collective-permute-start(f32[8,1152]{1,0:T(8,128)S(1)} %get-tuple-element.9), channel_id=1, source_target_pairs={{0,64},{64,0},{128,192},{192,128},{256,320},{320,256},{384,448},{4... | collective-permute-start | bytes 110600 | tf_op jit(solution)/shard_map/ppermute | solution.py:286
  10.3 1.9 %collective-permute-start.1 = (f32[8,1152]{1,0:T(8,128)S(1)}, f32[8,1152]{1,0:T(8,128)S(1)}, u32[]{:S(2)}, u32[]{:S(2)}) collective-permute-start(f32[8,1152]{1,0:T(8,128)S(1)} %get-tuple-element.10), channel_id=1, source_target_pairs={{64,128},{128,64},{192,256},{256,192},{320,384},{384,320},{65,129}... | collective-permute-start | bytes 110600 | tf_op jit(solution)/shard_map/ppermute | solution.py:285
  12.2 1.7 %table.1.table_ref = bf16[48,128,256]{2,1,0:T(8,128)(2,1)S(1)} custom-call(f32[16,128,128]{2,1,0:T(8,128)} %tiles_ref.1), custom_call_target="tpu_custom_call" | custom-call | tf_op jit(solution)/shard_map/table/pallas_call | solution.py:288
  13.9 0.0 collective-permute-done.mate_ref
  13.9 1.7 %collective-permute-done.1.cross_ref = f32[8,1152]{1,0:T(8,128)S(1)} collective-permute-done((f32[8,1152]{1,0:T(8,128)S(1)}, f32[8,1152]{1,0:T(8,128)S(1)}, u32[]{:S(2)}, u32[]{:S(2)}) %collective-permute-start.1) | collective-permute-done | bytes 36896 | tf_op jit(solution)/shard_map/ppermute | solution.py:285
  15.6 0.0 copy-done
  15.6 0.0 copy-done.1
  15.6 5.6 %filter.1 = (f32[8,4096]{1,0:T(8,128)S(1)}, f32[64,8,256]{2,1,0:T(8,128)S(1)}) custom-call(f32[8,4096]{1,0:T(8,128)S(1)} %copy-done, f32[8,1152]{1,0:T(8,128)S(1)} %collective-permute-done.mate_ref, f32[8,1152]{1,0:T(8,128)S(1)} %collective-permute-done.1.cross_ref, f32[8,128]{1,0:T(8,128)S(1)} %get-tuple-element.11.own_ref, ...), custom_call_target="tpu_custom_call" | custom-call | tf_op jit(solution)/shard_map/filter/pallas_call | solution.py:303
  21.2 24.6 %all_to_all.10 = f32[64,8,256]{2,1,0:T(8,128)S(1)} all-to-all(f32[64,8,256]{2,1,0:T(8,128)S(1)} %get-tuple-element.12), channel_id=1, replica_groups={{43,42,41,40,47,46,45,44,35,34,33,32,39,38,37,36,59,58,57,56,63,62,61,6..., dimensions={0} | all-to-all | bytes 1048576 | tf_op jit(solution)/shard_map/all_to_all | solution.py:321
  45.8 0.7 %gram.1 = (f32[512,128]{1,0:T(8,128)S(1)}, f32[8,4096]{1,0:T(8,128)}) custom-call(f32[512,256]{1,0:T(8,128)S(1)} %bitcast.6, f32[8,4096]{1,0:T(8,128)S(1)} %get-tuple-element.13.filtered_ref), custom_call_target="tpu_custom_call" | custom-call | tf_op jit(solution)/shard_map/gram/pallas_call | solution.py:332
  46.6 21.8 %all_to_all.11 = f32[128,1,512]{2,1,0:T(1,128)S(1)} all-to-all(f32[128,1,512]{2,1,0:T(1,128)S(1)} %bitcast.8), channel_id=1, replica_groups={{225,224,227,226,241,240,243,242,193,192,195,194,209,208,211,210,161,16..., dimensions={0} | all-to-all | bytes 524288 | tf_op jit(solution)/shard_map/all_to_all | solution.py:346
  68.3 0.6 sum.1
Async XLA Ops:
  0.6 15.0 %copy-start = (f32[8,4096]{1,0:T(8,128)S(1)}, f32[8,4096]{1,0:T(8,128)}, u32[]{:S(2)}) copy-start(f32[8,4096]{1,0:T(8,128)} %vectors_ref.3) | copy-start | bytes 393220
  0.6 15.0 %copy-start.1 = (f32[3]{0:T(128)S(1)}, f32[3]{0:T(128)}, u32[]{:S(2)}) copy-start(f32[3]{0:T(128)} %bounds_ref.1) | copy-start | bytes 40
  1.6 12.4 %collective-permute-start = (f32[8,1152]{1,0:T(8,128)S(1)}, f32[8,1152]{1,0:T(8,128)S(1)}, u32[]{:S(2)}, u32[]{:S(2)}) collective-permute-start(f32[8,1152]{1,0:T(8,128)S(1)} %get-tuple-element.9), channel_id=1, source_target_pairs={{0,64},{64,0},{128,192},{192,128},{256,320},{320,256},{384,448},{4... | collective-permute-start | bytes 110600 | tf_op jit(solution)/shard_map/ppermute | solution.py:286
  10.3 5.3 %collective-permute-start.1 = (f32[8,1152]{1,0:T(8,128)S(1)}, f32[8,1152]{1,0:T(8,128)S(1)}, u32[]{:S(2)}, u32[]{:S(2)}) collective-permute-start(f32[8,1152]{1,0:T(8,128)S(1)} %get-tuple-element.10), channel_id=1, source_target_pairs={{64,128},{128,64},{192,256},{256,192},{320,384},{384,320},{65,129}... | collective-permute-start | bytes 110600 | tf_op jit(solution)/shard_map/ppermute | solution.py:285
